TPU v7x, 32 devices: a whole 2x2x4 slice. The times are simulated.
32 devices in a mesh: ctx: 8 (over z, y), head: 4 (over x, core).
Axes of the slice: x: 2, y: 2, z: 4, core: 2. Of those that a mesh axis runs over, the one named last changes fastest.
Arguments:
- queries: bfloat16 [3072, 2048], P('ctx', 'head'), may hold values from -10 to 10, as said below
- key_rows: bfloat16 [3072, 2048], P('ctx', 'head'), may hold values from -10 to 10, as said below
- value_rows: bfloat16 [3072, 2048], P('ctx', 'head'), may hold values from -6 to 6
- out_weight: bfloat16 [2048, 2048], P('head'), may hold values from -0.125 to 0.125
- cotangent: bfloat16 [3072, 2048], P('ctx', 'head'), may hold values from -6 to 6
- offsets: int32 [136], replicated, may hold values from 0 to 25920, as said below
Outputs:
- mixed: bfloat16 [3072, 2048], P('ctx', 'head')
- grad_queries: bfloat16 [3072, 2048], P('ctx', 'head')
- grad_keys: bfloat16 [3072, 2048], P('ctx', 'head')
- grad_values: bfloat16 [3072, 2048], P('ctx', 'head')
Inputs may be any that keep to these rules, and one draw needn't show every extreme that they name: offsets start at 0 and increase; consecutive entries differ by 1 to 192 except before the last entry, which is (135) * 192 and lies beyond the history, as does the entry before it. `queries`: real values. `key_rows`: real values.
All inputs are finite; a program needn't handle non-finite values.
Results may differ from a plain program's by a relative error of at most 0.018.
Values may be sent and summed in bfloat16 or wider, within the bound.
No kernel may reach another device: no remote copies, remote signals or barrier semaphores. Data moves between devices by JAX's collectives and lax.ppermute only.
A program may use at most 64 MiB of HBM per device.

v0:
```python
import functools
import math

import jax
import jax.numpy as jnp
from jax import lax
from jax.experimental import pallas as pl
from jax.experimental.pallas import tpu as pltpu
from jax.sharding import PartitionSpec as P


HD = 128
REACH = 2
PREV = 3
ROWS = 128
NEG_FILL = -1e30
SCALE = 1.0 / math.sqrt(HD)
LOG2E = 1.4426950408889634
VMEM_BYTES = 67043328
F32 = jnp.float32
BF16 = jnp.bfloat16


NT = (((1,), (1,)), ((), ()))
NN = (((1,), (0,)), ((), ()))


def passed_along(shard, axis, by):
    length = lax.axis_size(axis)
    pairs = [(i, i + by) for i in range(length) if 0 <= i + by < length]
    return lax.ppermute(shard, axis, pairs)


def swapped(shard, axis, bit):
    length = lax.axis_size(axis)
    return lax.ppermute(shard, axis, [(i, i ^ bit) for i in range(length)])


def window_starts(positions, offsets):
    later, first = offsets[PREV:], offsets[:-PREV]
    reached = jnp.where(later[None, :] <= positions[:, None], first[None, :], 0)
    return jnp.max(reached, axis=1)


def mm(a, b, dims):
    return lax.dot_general(a, b, dims, preferred_element_type=F32)


def grad_out_kernel(me_ref, c0, c1, c2, c3, w_ref, out_ref):
    cols = c0.shape[1]
    total = None
    for s, c in enumerate((c0, c1, c2, c3)):
        start = pl.multiple_of((me_ref[0] ^ s) * cols, cols)
        part = mm(c[...], w_ref[:, pl.ds(start, cols)], NT)
        total = part if total is None else total + part
    out_ref[...] = total.astype(BF16)


def grad_out_call(me, shards, weight):
    rows, cols = shards[0].shape
    whole = pl.BlockSpec((rows, cols), lambda h, me: (0, 0))
    return pl.pallas_call(
        grad_out_kernel,
        name="grad_out",
        out_shape=jax.ShapeDtypeStruct((rows, cols), BF16),
        grid_spec=pltpu.PrefetchScalarGridSpec(
            num_scalar_prefetch=1,
            grid=(cols // HD,),
            in_specs=[whole] * 4 + [pl.BlockSpec((HD, weight.shape[1]), lambda h, me: (h, 0))],
            out_specs=pl.BlockSpec((rows, HD), lambda h, me: (0, h)),
        ),
        compiler_params=pltpu.CompilerParams(vmem_limit_bytes=VMEM_BYTES),
        cost_estimate=pl.CostEstimate(
            flops=2 * rows * cols * weight.shape[1], bytes_accessed=6 << 20, transcendentals=0
        ),
    )(me, *shards, weight)


def key_pieces(block, rows):
    first, last = block * ROWS, (block + 1) * ROWS
    return ((2, first, rows, -2 * rows), (1, 0, rows, -rows), (0, 0, last, 0))


def pick(odd, even_ref, odd_ref, into):
    @pl.when(odd == 0)
    def _():
        into[...] = even_ref[...]

    @pl.when(odd == 1)
    def _():
        into[...] = odd_ref[...]


def attend_kernel(odd_ref, lo_ref, q, k0, k2, v0, v2, r1, r2, r3, g, att_ref, prob_ref, stat_ref, k1, v1):
    rows = q.shape[0]
    pick(odd_ref[0], r2, r1, k1)
    pick(odd_ref[0], r3, r2, v1)
    keys, values = (k0, k1, k2), (v0, v1, v2)
    for b in range(rows // ROWS):
        mine = slice(b * ROWS, (b + 1) * ROWS)
        qb = q[mine, :]
        lo = lo_ref[mine, :]
        scores = []
        for tile, first, last, off in key_pieces(b, rows):
            raw = mm(qb, keys[tile][first:last, :], NT)
            pos = off + first + lax.broadcasted_iota(jnp.int32, raw.shape, 1)
            ok = pos >= lo
            if tile == 0:
                ok &= pos <= b * ROWS + lax.broadcasted_iota(jnp.int32, raw.shape, 0)
            scores.append(jnp.where(ok, raw, NEG_FILL))
        top = functools.reduce(
            jnp.maximum, [jnp.max(s, axis=1, keepdims=True) for s in scores]
        )
        shift = top * (SCALE * LOG2E)
        exps = [jnp.exp2(s * (SCALE * LOG2E) - shift) for s in scores]
        total = functools.reduce(jnp.add, [jnp.sum(e, axis=1, keepdims=True) for e in exps])
        inverse = 1.0 / total
        mixed = None
        column = 0
        for e, (tile, first, last, off) in zip(exps, key_pieces(b, rows)):
            prob = (e * inverse).astype(BF16)
            prob_ref[0, mine, column : column + last - first] = prob
            column += last - first
            part = mm(prob, values[tile][first:last, :], NN)
            mixed = part if mixed is None else mixed + part
        attended = mixed.astype(BF16)
        att_ref[mine, :] = attended
        delta = jnp.sum(attended.astype(F32) * g[mine, :].astype(F32), axis=1, keepdims=True)
        log_total = shift + jnp.log2(total)
        lane = lax.broadcasted_iota(jnp.int32, (ROWS, ROWS), 1)
        stats = jnp.where(lane == 0, log_total, delta).T
        stat_ref[0, :, mine] = stats[0:2, :]


def tile_specs(rows):
    tile = pl.BlockSpec((rows, HD), lambda h, odd: (0, h))
    on_odd = pl.BlockSpec((rows, HD), lambda h, odd: (0, h * odd[0]))
    on_even = pl.BlockSpec((rows, HD), lambda h, odd: (0, h * (1 - odd[0])))
    return tile, on_odd, on_even


def attend_call(odd, lo, q, k0, k2, v0, v2, r1, r2, r3, g):
    rows, cols = q.shape
    heads = cols // HD
    tile, on_odd, on_even = tile_specs(rows)
    span = REACH * rows + ROWS
    return pl.pallas_call(
        attend_kernel,
        name="attend",
        out_shape=(
            jax.ShapeDtypeStruct((rows, cols), BF16),
            jax.ShapeDtypeStruct((heads, rows, span), BF16),
            jax.ShapeDtypeStruct((heads, 2, rows), F32),
        ),
        grid_spec=pltpu.PrefetchScalarGridSpec(
            num_scalar_prefetch=1,
            grid=(heads,),
            in_specs=[pl.BlockSpec((rows, 1), lambda h, odd: (0, 0))]
            + [tile] * 5
            + [on_odd, tile, on_even, tile],
            out_specs=(
                tile,
                pl.BlockSpec((1, rows, span), lambda h, odd: (h, 0, 0)),
                pl.BlockSpec((1, 2, rows), lambda h, odd: (h, 0, 0)),
            ),
            scratch_shapes=[pltpu.VMEM((rows, HD), BF16)] * 2,
        ),
        compiler_params=pltpu.CompilerParams(vmem_limit_bytes=VMEM_BYTES),
        cost_estimate=pl.CostEstimate(
            flops=4 * heads * rows * span * HD, bytes_accessed=8 << 20,
            transcendentals=heads * rows * span,
        ),
    )(odd, lo, q, k0, k2, v0, v2, r1, r2, r3, g)


def project_kernel(me_ref, a_ref, w_ref, out_ref):
    out_ref[...] = mm(a_ref[...], w_ref[...], NN).astype(out_ref.dtype)


def project_call(me, attended, weight, swaps, dtype):
    rows, cols = attended.shape
    base, step = swaps

    return pl.pallas_call(
        project_kernel,
        name="project",
        out_shape=jax.ShapeDtypeStruct((rows, 2 * cols), dtype),
        grid_spec=pltpu.PrefetchScalarGridSpec(
            num_scalar_prefetch=1,
            grid=(2,),
            in_specs=[
                pl.BlockSpec((rows, cols), lambda s, me: (0, 0)),
                pl.BlockSpec((cols, cols), lambda s, me: (0, me[0] ^ (base + step * s))),
            ],
            out_specs=pl.BlockSpec((rows, cols), lambda s, me: (0, s)),
        ),
        compiler_params=pltpu.CompilerParams(vmem_limit_bytes=VMEM_BYTES),
        cost_estimate=pl.CostEstimate(
            flops=4 * rows * cols * cols, bytes_accessed=3 << 20, transcendentals=0
        ),
    )(me, attended, weight)


def query_grad_kernel(odd_ref, prob_ref, att, k0, k2, v0, v2, r1, r2, r3, g, out_ref, k1, v1):
    rows = g.shape[0]
    pick(odd_ref[0], r2, r1, k1)
    pick(odd_ref[0], r3, r2, v1)
    keys, values = (k0, k1, k2), (v0, v1, v2)
    for b in range(rows // ROWS):
        mine = slice(b * ROWS, (b + 1) * ROWS)
        gb = g[mine, :]
        delta = jnp.sum(att[mine, :].astype(F32) * gb.astype(F32), axis=1, keepdims=True)
        total = None
        column = 0
        for tile, first, last, off in key_pieces(b, rows):
            prob = prob_ref[0, mine, column : column + last - first].astype(F32)
            column += last - first
            grad_prob = mm(gb, values[tile][first:last, :], NT)
            grad_score = (prob * (grad_prob - delta)).astype(BF16)
            part = mm(grad_score, keys[tile][first:last, :], NN)
            total = part if total is None else total + part
        out_ref[mine, :] = (total * SCALE).astype(BF16)


def query_grad_call(odd, prob, att, k0, k2, v0, v2, r1, r2, r3, g):
    rows, cols = g.shape
    heads = cols // HD
    tile, on_odd, on_even = tile_specs(rows)
    span = REACH * rows + ROWS
    return pl.pallas_call(
        query_grad_kernel,
        name="query_grad",
        out_shape=jax.ShapeDtypeStruct((rows, cols), BF16),
        grid_spec=pltpu.PrefetchScalarGridSpec(
            num_scalar_prefetch=1,
            grid=(heads,),
            in_specs=[pl.BlockSpec((1, rows, span), lambda h, odd: (h, 0, 0))]
            + [tile] * 5
            + [on_odd, tile, on_even, tile],
            out_specs=tile,
            scratch_shapes=[pltpu.VMEM((rows, HD), BF16)] * 2,
        ),
        compiler_params=pltpu.CompilerParams(vmem_limit_bytes=VMEM_BYTES),
        cost_estimate=pl.CostEstimate(
            flops=4 * heads * rows * span * HD, bytes_accessed=8 << 20, transcendentals=0
        ),
    )(odd, prob, att, k0, k2, v0, v2, r1, r2, r3, g)


def key_grad_kernel(
    odd_ref, lo_ref, k, v, q0, q2, r1, r3, g0, g1, g2, s0, s1, s2, dk_ref, dv_ref, q1
):
    rows = k.shape[0]
    pick(odd_ref[0], r1, r3, q1)
    queries, grads, stats = (q0, q1, q2), (g0, g1, g2), (s0, s1, s2)
    for b in range(rows // ROWS):
        mine = slice(b * ROWS, (b + 1) * ROWS)
        kb, vb = k[mine, :], v[mine, :]
        dk = dv = None
        pieces = ((0, b * ROWS, rows), (1, 0, rows), (2, 0, (b + 1) * ROWS))
        for tile, first, last in pieces:
            qt, gt = queries[tile][first:last, :], grads[tile][first:last, :]
            raw = mm(kb, qt, NT)
            pos = b * ROWS + lax.broadcasted_iota(jnp.int32, raw.shape, 0)
            ok = pos >= lo_ref[tile : tile + 1, first:last]
            if tile == 0:
                ok &= pos <= first + lax.broadcasted_iota(jnp.int32, raw.shape, 1)
            log_total = stats[tile][0, 0:1, first:last]
            delta = stats[tile][0, 1:2, first:last]
            prob = jnp.where(ok, jnp.exp2(raw * (SCALE * LOG2E) - log_total), 0.0)
            grad_prob = mm(vb, gt, NT)
            grad_score = (prob * (grad_prob - delta)).astype(BF16)
            part_k = mm(grad_score, qt, NN)
            part_v = mm(prob.astype(BF16), gt, NN)
            dk = part_k if dk is None else dk + part_k
            dv = part_v if dv is None else dv + part_v
        dk_ref[mine, :] = (dk * SCALE).astype(BF16)
        dv_ref[mine, :] = dv.astype(BF16)


def key_grad_call(odd, lo, k, v, q0, q2, r1, r3, grads, stats):
    rows, cols = k.shape
    heads = cols // HD
    tile, on_odd, on_even = tile_specs(rows)
    stat = pl.BlockSpec((1, 2, rows), lambda h, odd: (h, 0, 0))
    span = REACH * rows + ROWS
    return pl.pallas_call(
        key_grad_kernel,
        name="key_grad",
        out_shape=(jax.ShapeDtypeStruct((rows, cols), BF16),) * 2,
        grid_spec=pltpu.PrefetchScalarGridSpec(
            num_scalar_prefetch=1,
            grid=(heads,),
            in_specs=[pl.BlockSpec((REACH + 1, rows), lambda h, odd: (0, 0))]
            + [tile] * 4
            + [on_even, on_odd]
            + [tile] * 3
            + [stat] * 3,
            out_specs=(tile, tile),
            scratch_shapes=[pltpu.VMEM((rows, HD), BF16)],
        ),
        compiler_params=pltpu.CompilerParams(vmem_limit_bytes=VMEM_BYTES),
        cost_estimate=pl.CostEstimate(
            flops=8 * heads * rows * span * HD, bytes_accessed=5 << 20,
            transcendentals=heads * rows * span,
        ),
    )(odd, lo, k, v, q0, q2, r1, r3, *grads, *stats)


def layer(queries, key_rows, value_rows, out_weight, cotangent, offsets):
    rows, cols = queries.shape
    count = lax.axis_size("ctx")
    index = lax.axis_index("ctx")
    base = index * rows
    odd = (index % 2).astype(jnp.int32).reshape(1)
    me = lax.axis_index("head").astype(jnp.int32).reshape(1)

    def along(shard, by):
        return passed_along(shard, "ctx", by)

    def across(shard, bit):
        return swapped(shard, "head", bit)

    def pair(from_even, from_odd):
        return swapped(jnp.where(index % 2 == 0, from_even, from_odd), "ctx", 1)

    def turned(shard, by):
        return lax.ppermute(shard, "ctx", [(i, (i + by) % count) for i in range(count)])

    cot_far = across(cotangent, 2)
    cot_near = across(cotangent, 1)
    k2 = along(key_rows, 2)
    r1 = pair(key_rows, queries)
    q2 = along(queries, -2)
    v2 = along(value_rows, 2)
    cot_both = across(cot_far, 1)

    positions = base + jnp.arange((REACH + 1) * rows, dtype=jnp.int32)
    lo = window_starts(positions, offsets) - base
    lo = jnp.where(positions < count * rows, lo, (REACH + 1) * rows).reshape(REACH + 1, rows)

    g = grad_out_call(me, (cotangent, cot_near, cot_far, cot_both), out_weight)
    g2 = along(g, -2)
    r2 = pair(value_rows, k2)
    r3 = pair(q2, v2)
    g1 = pair(g2, g)

    attended, prob, stat = attend_call(
        odd, lo[0].reshape(rows, 1), queries, key_rows, k2, value_rows, v2, r1, r2, r3, g
    )
    stat1 = turned(stat, -1)
    stat2 = turned(stat, -2)

    sent = project_call(me, attended, out_weight, (1, 2), BF16)
    came = across(sent, 1)
    kept = project_call(me, attended, out_weight, (0, 2), F32)
    both = kept + came.astype(F32)
    mine, other = both[:, :cols], both[:, cols:].astype(BF16)
    far = across(other, 2)
    grad_queries = query_grad_call(
        odd, prob, attended, key_rows, k2, value_rows, v2, r1, r2, r3, g
    )
    grad_keys, grad_values = key_grad_call(
        odd, lo, key_rows, value_rows, queries, q2, r1, r3, (g, g1, g2), (stat, stat1, stat2)
    )
    mixed = (mine + far.astype(F32)).astype(BF16)
    return (mixed, grad_queries, grad_keys, grad_values)


def solution(mesh):
    in_specs = (
        P("ctx", "head"),
        P("ctx", "head"),
        P("ctx", "head"),
        P("head", None),
        P("ctx", "head"),
        P(),
    )
    out_specs = (P("ctx", "head"), P("ctx", "head"), P("ctx", "head"), P("ctx", "head"))
    return jax.shard_map(layer, mesh=mesh, in_specs=in_specs, out_specs=out_specs, check_vma=False)
```

profile of v0, /device:TPU:0, one launch (start us, length us, event | category | flops | bytes accessed | tf_op | source)
XLA Modules:
  0.0 102.4 jit_solution(13976659207513138980)
XLA Ops:
  1.2 2.6 %collective-permute-start.7 = (bf16[384,512]{1,0:T(8,128)(2,1)}, bf16[384,512]{1,0:T(8,128)(2,1)S(1)}, u32[]{:S(2)}, u32[]{:S(2)}) collective-permute-start(bf16[384,512]{1,0:T(8,128)(2,1)} %c0.1), channel_id=1, source_target_pairs={{0,2},{1,3},{2,0},{3,1},{4,6},{5,7},{6,4},{7,5},{8,10},{9,11},{10,... | collective-permute-start | bytes 1179656 | tf_op jit(solution)/shard_map/ppermute | solution.py:36
  3.7 1.3 %collective-permute-start.4 = (bf16[384,512]{1,0:T(8,128)(2,1)}, bf16[384,512]{1,0:T(8,128)(2,1)S(1)}, u32[]{:S(2)}, u32[]{:S(2)}) collective-permute-start(bf16[384,512]{1,0:T(8,128)(2,1)} %q0.1), channel_id=1, source_target_pairs={{8,0},{12,4},{16,8},{20,12},{24,16},{28,20},{9,1},{13,5},{17,9},{2... | collective-permute-start | bytes 1179656 | tf_op jit(solution)/shard_map/ppermute | solution.py:31
  5.0 4.6 %collective-permute-start = (bf16[384,512]{1,0:T(8,128)(2,1)}, bf16[384,512]{1,0:T(8,128)(2,1)S(1)}, u32[]{:S(2)}, u32[]{:S(2)}) collective-permute-start(bf16[384,512]{1,0:T(8,128)(2,1)} %k.1), channel_id=1, source_target_pairs={{0,8},{4,12},{8,16},{12,20},{16,24},{20,28},{1,9},{5,13},{9,17},{1... | collective-permute-start | bytes 1179656 | tf_op jit(solution)/shard_map/ppermute | solution.py:31
  9.6 3.5 %collective-permute-start.1 = (bf16[384,512]{1,0:T(8,128)(2,1)}, bf16[384,512]{1,0:T(8,128)(2,1)S(1)}, u32[]{:S(2)}, u32[]{:S(2)}) collective-permute-start(bf16[384,512]{1,0:T(8,128)(2,1)} %v.1), channel_id=1, source_target_pairs={{0,8},{4,12},{8,16},{12,20},{16,24},{20,28},{1,9},{5,13},{9,17},{1... | collective-permute-start | bytes 1179656 | tf_op jit(solution)/shard_map/ppermute | solution.py:31
  13.1 1.8 %broadcast_select_fusion.3 = bf16[384,512]{1,0:T(8,128)(2,1)} fusion(bf16[384,512]{1,0:T(8,128)(2,1)} %k.1, bf16[384,512]{1,0:T(8,128)(2,1)} %q0.1, pred[]{:T(512)S(6)} %eq.12), kind=kLoop, calls=%fused_computation.8 | loop fusion | flops 196608 | bytes 1179649 | tf_op jit(solution)/shard_map/jit(_where)/select_n | solution.py:325
  14.9 0.8 fusion.2
  15.9 3.5 %collective-permute-done.k2 = bf16[384,512]{1,0:T(8,128)(2,1)S(1)} collective-permute-done((bf16[384,512]{1,0:T(8,128)(2,1)}, bf16[384,512]{1,0:T(8,128)(2,1)S(1)}, u32[]{:S(2)}, u32[]{:S(2)}) %collective-permute-start) | collective-permute-done | bytes 393248 | tf_op jit(solution)/shard_map/ppermute | solution.py:31
  19.4 1.5 %collective-permute-start.2 = (bf16[384,512]{1,0:T(8,128)(2,1)}, bf16[384,512]{1,0:T(8,128)(2,1)}, u32[]{:S(2)}, u32[]{:S(2)}) collective-permute-start(bf16[384,512]{1,0:T(8,128)(2,1)} %broadcast_select_fusion.3), channel_id=1, source_target_pairs={{0,4},{4,0},{8,12},{12,8},{16,20},{20,16},{24,28},{28,24},{1,5},{5... | collective-permute-start | bytes 1179656 | tf_op jit(solution)/shard_map/ppermute | solution.py:36
  20.9 1.8 %broadcast_select_fusion.2 = bf16[384,512]{1,0:T(8,128)(2,1)} fusion(bf16[384,512]{1,0:T(8,128)(2,1)} %v.1, bf16[384,512]{1,0:T(8,128)(2,1)S(1)} %collective-permute-done.k2, pred[]{:T(512)S(6)} %eq.12), kind=kLoop, calls=%fused_computation.7 | loop fusion | flops 196608 | bytes 1179649 | tf_op jit(solution)/shard_map/jit(_where)/select_n | solution.py:325
  22.7 4.0 %collective-permute-done.1.v2 = bf16[384,512]{1,0:T(8,128)(2,1)S(1)} collective-permute-done((bf16[384,512]{1,0:T(8,128)(2,1)}, bf16[384,512]{1,0:T(8,128)(2,1)S(1)}, u32[]{:S(2)}, u32[]{:S(2)}) %collective-permute-start.1) | collective-permute-done | bytes 393248 | tf_op jit(solution)/shard_map/ppermute | solution.py:31
  28.3 1.5 %collective-permute-start.5 = (bf16[384,512]{1,0:T(8,128)(2,1)}, bf16[384,512]{1,0:T(8,128)(2,1)}, u32[]{:S(2)}, u32[]{:S(2)}) collective-permute-start(bf16[384,512]{1,0:T(8,128)(2,1)} %broadcast_select_fusion.1), channel_id=1, source_target_pairs={{0,4},{4,0},{8,12},{12,8},{16,20},{20,16},{24,28},{28,24},{1,5},{5... | collective-permute-start | bytes 1179656 | tf_op jit(solution)/shard_map/ppermute | solution.py:36
  30.6 0.8 reshape_squeeze.4.lo_ref
  31.4 0.9 collective-permute-done.8.c3
  33.0 5.0 %grad_out.1.g.g0 = bf16[384,512]{1,0:T(8,128)(2,1)} custom-call(s32[1]{0:T(128)} %bitcast.me_ref, bf16[384,512]{1,0:T(8,128)(2,1)} %c0.1, bf16[384,512]{1,0:T(8,128)(2,1)} %collective-permute-done.6.c1, bf16[384,512]{1,0:T(8,128)(2,1)} %copy-done.3, bf16[384,512]{1,0:T(8,128)(2,1)} %copy-done.4, bf16[512,2048]{1,0:T(8,128)(2,1)} %w_ref.5), custom_call_target="tpu_custom_call" | custom-call | flops 805306368 | bytes 6291456 | tf_op jit(solution)/shard_map/grad_out/pallas_call | solution.py:62
  38.1 2.1 %collective-permute-done.3.r2 = bf16[384,512]{1,0:T(8,128)(2,1)} collective-permute-done((bf16[384,512]{1,0:T(8,128)(2,1)}, bf16[384,512]{1,0:T(8,128)(2,1)}, u32[]{:S(2)}, u32[]{:S(2)}) %collective-permute-start.3) | collective-permute-done | bytes 393248 | tf_op jit(solution)/shard_map/ppermute | solution.py:36
  40.1 5.4 %collective-permute-done.5.r3 = bf16[384,512]{1,0:T(8,128)(2,1)} collective-permute-done((bf16[384,512]{1,0:T(8,128)(2,1)}, bf16[384,512]{1,0:T(8,128)(2,1)}, u32[]{:S(2)}, u32[]{:S(2)}) %collective-permute-start.5) | collective-permute-done | bytes 393248 | tf_op jit(solution)/shard_map/ppermute | solution.py:36
  45.5 9.0 %attend.1 = (bf16[384,512]{1,0:T(8,128)(2,1)}, bf16[4,384,896]{2,1,0:T(8,128)(2,1)}, f32[4,2,384]{2,1,0:T(2,128)}) custom-call(s32[1]{0:T(128)} %bitcast.1.odd_ref, s32[384,1]{1,0:T(8,128)} %reshape_squeeze.4.lo_ref, bf16[384,512]{1,0:T(8,128)(2,1)} %q0.1, bf16[384,512]{1,0:T(8,128)(2,1)} %k.1, bf16[384,512]{1,0:T(8,128)(2,1)} %copy-done.1, ...), custom_call_target="tpu_custom_call" | custom-call | flops 704643072 | bytes 8388608 | tf_op jit(solution)/shard_map/attend/pallas_call | solution.py:147
  54.5 2.8 %project.3 = bf16[384,1024]{1,0:T(8,128)(2,1)} custom-call(s32[1]{0:T(128)} %bitcast.me_ref, bf16[384,512]{1,0:T(8,128)(2,1)} %get-tuple-element.9.a_ref.att, bf16[512,2048]{1,0:T(8,128)(2,1)} %w_ref.5), custom_call_target="tpu_custom_call" | custom-call | flops 402653184 | bytes 3145728 | tf_op jit(solution)/shard_map/project/pallas_call | solution.py:184
  57.3 1.3 %collective-permute-start.11 = (bf16[384,512]{1,0:T(8,128)(2,1)}, bf16[384,512]{1,0:T(8,128)(2,1)}, u32[]{:S(2)}, u32[]{:S(2)}) collective-permute-start(bf16[384,512]{1,0:T(8,128)(2,1)} %grad_out.1.g.g0), channel_id=1, source_target_pairs={{8,0},{12,4},{16,8},{20,12},{24,16},{28,20},{9,1},{13,5},{17,9},{2... | collective-permute-start | bytes 1179656 | tf_op jit(solution)/shard_map/ppermute | solution.py:31
  58.6 1.3 %sub.9 = s32[3,384]{1,0:T(4,128)} reshape(s32[1152]{0:T(1024)} %copy-done.6) | data formatting | bytes 9216 | tf_op jit(solution)/shard_map/sub | solution.py:339
  59.9 2.9 %project.2 = f32[384,1024]{1,0:T(8,128)} custom-call(s32[1]{0:T(128)} %bitcast.me_ref, bf16[384,512]{1,0:T(8,128)(2,1)} %get-tuple-element.9.a_ref.att, bf16[512,2048]{1,0:T(8,128)(2,1)} %w_ref.5), custom_call_target="tpu_custom_call" | custom-call | flops 402653184 | bytes 3145728 | tf_op jit(solution)/shard_map/project/pallas_call | solution.py:184
  62.7 8.9 %collective-permute-done.11.g2 = bf16[384,512]{1,0:T(8,128)(2,1)} collective-permute-done((bf16[384,512]{1,0:T(8,128)(2,1)}, bf16[384,512]{1,0:T(8,128)(2,1)}, u32[]{:S(2)}, u32[]{:S(2)}) %collective-permute-start.11) | collective-permute-done | bytes 393248 | tf_op jit(solution)/shard_map/ppermute | solution.py:31
  71.7 1.8 %broadcast_select_fusion = bf16[384,512]{1,0:T(8,128)(2,1)} fusion(bf16[384,512]{1,0:T(8,128)(2,1)} %collective-permute-done.11.g2, bf16[384,512]{1,0:T(8,128)(2,1)} %grad_out.1.g.g0, pred[]{:T(512)S(6)} %eq.12), kind=kLoop, calls=%fused_computation.5 | loop fusion | flops 196608 | bytes 1179649 | tf_op jit(solution)/shard_map/jit(_where)/select_n | solution.py:325
  73.5 1.5 %collective-permute-start.12 = (bf16[384,512]{1,0:T(8,128)(2,1)}, bf16[384,512]{1,0:T(8,128)(2,1)}, u32[]{:S(2)}, u32[]{:S(2)}) collective-permute-start(bf16[384,512]{1,0:T(8,128)(2,1)} %broadcast_select_fusion), channel_id=1, source_target_pairs={{0,4},{4,0},{8,12},{12,8},{16,20},{20,16},{24,28},{28,24},{1,5},{5... | collective-permute-start | bytes 1179656 | tf_op jit(solution)/shard_map/ppermute | solution.py:36
  75.0 1.8 %convert_add_fusion = f32[384,1024]{1,0:T(8,128)S(1)} fusion(f32[384,1024]{1,0:T(8,128)} %project.2, bf16[384,1024]{1,0:T(8,128)(2,1)} %collective-permute-done.9), kind=kLoop, calls=%fused_computation | loop fusion | flops 786432 | bytes 3932160 | tf_op jit(solution)/shard_map/add | solution.py:357
  76.9 1.1 %copy-done = f32[384,1024]{1,0:T(8,128)} copy-done((f32[384,1024]{1,0:T(8,128)}, f32[384,1024]{1,0:T(8,128)S(1)}, u32[]{:S(2)}) %copy-start) | copy-done | bytes 1572888
  78.0 0.8 slice.34
  79.9 1.7 %collective-permute-start.14 = (f32[4,2,384]{2,1,0:T(2,128)}, f32[4,2,384]{2,1,0:T(2,128)}, u32[]{:S(2)}, u32[]{:S(2)}) collective-permute-start(f32[4,2,384]{2,1,0:T(2,128)} %get-tuple-element.11.s0), channel_id=1, source_target_pairs={{0,24},{4,28},{8,0},{12,4},{16,8},{20,12},{24,16},{28,20},{1,25},{... | collective-permute-start | bytes 36872 | tf_op jit(solution)/shard_map/ppermute | solution.py:328
  81.7 2.4 %collective-permute-start.13 = (f32[4,2,384]{2,1,0:T(2,128)}, f32[4,2,384]{2,1,0:T(2,128)}, u32[]{:S(2)}, u32[]{:S(2)}) collective-permute-start(f32[4,2,384]{2,1,0:T(2,128)} %get-tuple-element.11.s0), channel_id=1, source_target_pairs={{0,28},{4,0},{8,4},{12,8},{16,12},{20,16},{24,20},{28,24},{1,29},{... | collective-permute-start | bytes 36872 | tf_op jit(solution)/shard_map/ppermute | solution.py:328
  84.1 6.9 %query_grad.1 = bf16[384,512]{1,0:T(8,128)(2,1)} custom-call(s32[1]{0:T(128)} %bitcast.1.odd_ref, bf16[4,384,896]{2,1,0:T(8,128)(2,1)} %get-tuple-element.10.prob_ref, bf16[384,512]{1,0:T(8,128)(2,1)} %get-tuple-element.9.a_ref.att, bf16[384,512]{1,0:T(8,128)(2,1)} %k.1, bf16[384,512]{1,0:T(8,128)(2,1)} %copy-done.1, bf16[384,512]{1,0:T(8,128)(2,1)} %v.1, ...), custom_call_target="tpu_custom_call" | custom-call | flops 704643072 | bytes 8388608 | tf_op jit(solution)/shard_map/query_grad/pallas_call | solution.py:230
  91.0 9.3 %key_grad.1 = (bf16[384,512]{1,0:T(8,128)(2,1)}, bf16[384,512]{1,0:T(8,128)(2,1)}) custom-call(s32[1]{0:T(128)} %bitcast.1.odd_ref, s32[3,384]{1,0:T(4,128)} %fusion.1.lo_ref, bf16[384,512]{1,0:T(8,128)(2,1)} %k.1, bf16[384,512]{1,0:T(8,128)(2,1)} %v.1, bf16[384,512]{1,0:T(8,128)(2,1)} %q0.1, bf16[384,512]{1,0:T(8,128)(2,1)} %copy-done.5, ...), custom_call_target="tpu_custom_call" | custom-call | flops 1409286144 | bytes 5242880 | tf_op jit(solution)/shard_map/key_grad/pallas_call | solution.py:287
  100.3 2.1 %fusion = bf16[384,512]{1,0:T(8,128)(2,1)} fusion(f32[384,1024]{1,0:T(8,128)} %copy-done, bf16[384,512]{1,0:T(8,128)(2,1)} %collective-permute-done.10), kind=kLoop, calls=%fused_computation.3 | loop fusion | flops 589824 | bytes 1572864 | tf_op jit(solution)/shard_map/convert_element_type | solution.py:366
  (35 shorter events, 5.0 us)
Async XLA Ops:
  0.6 30.7 %collective-permute-start.6 = (bf16[384,512]{1,0:T(8,128)(2,1)}, bf16[384,512]{1,0:T(8,128)(2,1)}, u32[]{:S(2)}, u32[]{:S(2)}) collective-permute-start(bf16[384,512]{1,0:T(8,128)(2,1)} %c0.1), channel_id=1, source_target_pairs={{0,1},{1,0},{2,3},{3,2},{4,5},{5,4},{6,7},{7,6},{8,9},{9,8},{10,11... | collective-permute-start | bytes 1179656 | tf_op jit(solution)/shard_map/ppermute | solution.py:36
  1.2 28.6 %collective-permute-start.7 = (bf16[384,512]{1,0:T(8,128)(2,1)}, bf16[384,512]{1,0:T(8,128)(2,1)S(1)}, u32[]{:S(2)}, u32[]{:S(2)}) collective-permute-start(bf16[384,512]{1,0:T(8,128)(2,1)} %c0.1), channel_id=1, source_target_pairs={{0,2},{1,3},{2,0},{3,1},{4,6},{5,7},{6,4},{7,5},{8,10},{9,11},{10,... | collective-permute-start | bytes 1179656 | tf_op jit(solution)/shard_map/ppermute | solution.py:36
  3.7 19.0 %collective-permute-start.4 = (bf16[384,512]{1,0:T(8,128)(2,1)}, bf16[384,512]{1,0:T(8,128)(2,1)S(1)}, u32[]{:S(2)}, u32[]{:S(2)}) collective-permute-start(bf16[384,512]{1,0:T(8,128)(2,1)} %q0.1), channel_id=1, source_target_pairs={{8,0},{12,4},{16,8},{20,12},{24,16},{28,20},{9,1},{13,5},{17,9},{2... | collective-permute-start | bytes 1179656 | tf_op jit(solution)/shard_map/ppermute | solution.py:31
  5.0 14.4 %collective-permute-start = (bf16[384,512]{1,0:T(8,128)(2,1)}, bf16[384,512]{1,0:T(8,128)(2,1)S(1)}, u32[]{:S(2)}, u32[]{:S(2)}) collective-permute-start(bf16[384,512]{1,0:T(8,128)(2,1)} %k.1), channel_id=1, source_target_pairs={{0,8},{4,12},{8,16},{12,20},{16,24},{20,28},{1,9},{5,13},{9,17},{1... | collective-permute-start | bytes 1179656 | tf_op jit(solution)/shard_map/ppermute | solution.py:31
  9.6 17.1 %collective-permute-start.1 = (bf16[384,512]{1,0:T(8,128)(2,1)}, bf16[384,512]{1,0:T(8,128)(2,1)S(1)}, u32[]{:S(2)}, u32[]{:S(2)}) collective-permute-start(bf16[384,512]{1,0:T(8,128)(2,1)} %v.1), channel_id=1, source_target_pairs={{0,8},{4,12},{8,16},{12,20},{16,24},{20,28},{1,9},{5,13},{9,17},{1... | collective-permute-start | bytes 1179656 | tf_op jit(solution)/shard_map/ppermute | solution.py:31
  19.4 1.5 %copy-start.1 = (bf16[384,512]{1,0:T(8,128)(2,1)}, bf16[384,512]{1,0:T(8,128)(2,1)S(1)}, u32[]{:S(2)}) copy-start(bf16[384,512]{1,0:T(8,128)(2,1)S(1)} %collective-permute-done.k2) | copy-start | bytes 1179652
  19.4 18.7 %collective-permute-start.2 = (bf16[384,512]{1,0:T(8,128)(2,1)}, bf16[384,512]{1,0:T(8,128)(2,1)}, u32[]{:S(2)}, u32[]{:S(2)}) collective-permute-start(bf16[384,512]{1,0:T(8,128)(2,1)} %broadcast_select_fusion.3), channel_id=1, source_target_pairs={{0,4},{4,0},{8,12},{12,8},{16,20},{20,16},{24,28},{28,24},{1,5},{5... | collective-permute-start | bytes 1179656 | tf_op jit(solution)/shard_map/ppermute | solution.py:36
  22.7 9.6 %copy-start.5 = (bf16[384,512]{1,0:T(8,128)(2,1)}, bf16[384,512]{1,0:T(8,128)(2,1)S(1)}, u32[]{:S(2)}) copy-start(bf16[384,512]{1,0:T(8,128)(2,1)S(1)} %collective-permute-done.4.q2) | copy-start | bytes 1179652
  22.7 17.4 %collective-permute-start.3 = (bf16[384,512]{1,0:T(8,128)(2,1)}, bf16[384,512]{1,0:T(8,128)(2,1)}, u32[]{:S(2)}, u32[]{:S(2)}) collective-permute-start(bf16[384,512]{1,0:T(8,128)(2,1)} %broadcast_select_fusion.2), channel_id=1, source_target_pairs={{0,4},{4,0},{8,12},{12,8},{16,20},{20,16},{24,28},{28,24},{1,5},{5... | collective-permute-start | bytes 1179656 | tf_op jit(solution)/shard_map/ppermute | solution.py:36
  26.7 0.7 copy-start.2
  28.3 17.2 %collective-permute-start.5 = (bf16[384,512]{1,0:T(8,128)(2,1)}, bf16[384,512]{1,0:T(8,128)(2,1)}, u32[]{:S(2)}, u32[]{:S(2)}) collective-permute-start(bf16[384,512]{1,0:T(8,128)(2,1)} %broadcast_select_fusion.1), channel_id=1, source_target_pairs={{0,4},{4,0},{8,12},{12,8},{16,20},{20,16},{24,28},{28,24},{1,5},{5... | collective-permute-start | bytes 1179656 | tf_op jit(solution)/shard_map/ppermute | solution.py:36
  29.8 0.8 copy-start.3
  30.6 1.7 %collective-permute-start.8 = (bf16[384,512]{1,0:T(8,128)(2,1)S(1)}, bf16[384,512]{1,0:T(8,128)(2,1)S(1)}, u32[]{:S(2)}, u32[]{:S(2)}) collective-permute-start(bf16[384,512]{1,0:T(8,128)(2,1)S(1)} %collective-permute-done.7.c2), channel_id=1, source_target_pairs={{0,1},{1,0},{2,3},{3,2},{4,5},{5,4},{6,7},{7,6},{8,9},{9,8},{10,11... | collective-permute-start | bytes 1179656 | tf_op jit(solution)/shard_map/ppermute | solution.py:36
  30.6 1.7 %copy-start.6 = (s32[1152]{0:T(1024)}, s32[1152]{0:T(1024)S(1)}, u32[]{:S(2)}) copy-start(s32[1152]{0:T(1024)S(1)} %broadcast_subtract_fusion) | copy-start | bytes 13828
  32.3 0.7 copy-start.4
  57.3 17.7 %collective-permute-start.9 = (bf16[384,1024]{1,0:T(8,128)(2,1)}, bf16[384,1024]{1,0:T(8,128)(2,1)}, u32[]{:S(2)}, u32[]{:S(2)}) collective-permute-start(bf16[384,1024]{1,0:T(8,128)(2,1)} %project.3), channel_id=1, source_target_pairs={{0,1},{1,0},{2,3},{3,2},{4,5},{5,4},{6,7},{7,6},{8,9},{9,8},{10,11... | collective-permute-start | bytes 2359304 | tf_op jit(solution)/shard_map/ppermute | solution.py:36
  57.3 14.4 %collective-permute-start.11 = (bf16[384,512]{1,0:T(8,128)(2,1)}, bf16[384,512]{1,0:T(8,128)(2,1)}, u32[]{:S(2)}, u32[]{:S(2)}) collective-permute-start(bf16[384,512]{1,0:T(8,128)(2,1)} %grad_out.1.g.g0), channel_id=1, source_target_pairs={{8,0},{12,4},{16,8},{20,12},{24,16},{28,20},{9,1},{13,5},{17,9},{2... | collective-permute-start | bytes 1179656 | tf_op jit(solution)/shard_map/ppermute | solution.py:31
  73.5 5.8 %copy-start.7 = (s32[3,384]{1,0:T(4,128)S(1)}, s32[3,384]{1,0:T(4,128)}, u32[]{:S(2)}) copy-start(s32[3,384]{1,0:T(4,128)} %sub.9) | copy-start | bytes 13828
  73.5 17.5 %collective-permute-start.12 = (bf16[384,512]{1,0:T(8,128)(2,1)}, bf16[384,512]{1,0:T(8,128)(2,1)}, u32[]{:S(2)}, u32[]{:S(2)}) collective-permute-start(bf16[384,512]{1,0:T(8,128)(2,1)} %broadcast_select_fusion), channel_id=1, source_target_pairs={{0,4},{4,0},{8,12},{12,8},{16,20},{20,16},{24,28},{28,24},{1,5},{5... | collective-permute-start | bytes 1179656 | tf_op jit(solution)/shard_map/ppermute | solution.py:36
  76.9 1.1 %copy-start = (f32[384,1024]{1,0:T(8,128)}, f32[384,1024]{1,0:T(8,128)S(1)}, u32[]{:S(2)}) copy-start(f32[384,1024]{1,0:T(8,128)S(1)} %convert_add_fusion) | copy-start | bytes 4718596
  78.8 21.5 %collective-permute-start.10 = (bf16[384,512]{1,0:T(8,128)(2,1)}, bf16[384,512]{1,0:T(8,128)(2,1)}, u32[]{:S(2)}, u32[]{:S(2)}) collective-permute-start(bf16[384,512]{1,0:T(8,128)(2,1)} %slice.34), channel_id=1, source_target_pairs={{0,2},{1,3},{2,0},{3,1},{4,6},{5,7},{6,4},{7,5},{8,10},{9,11},{10,... | collective-permute-start | bytes 1179656 | tf_op jit(solution)/shard_map/ppermute | solution.py:36
  79.9 11.1 %collective-permute-start.14 = (f32[4,2,384]{2,1,0:T(2,128)}, f32[4,2,384]{2,1,0:T(2,128)}, u32[]{:S(2)}, u32[]{:S(2)}) collective-permute-start(f32[4,2,384]{2,1,0:T(2,128)} %get-tuple-element.11.s0), channel_id=1, source_target_pairs={{0,24},{4,28},{8,0},{12,4},{16,8},{20,12},{24,16},{28,20},{1,25},{... | collective-permute-start | bytes 36872 | tf_op jit(solution)/shard_map/ppermute | solution.py:328
  81.7 9.3 %collective-permute-start.13 = (f32[4,2,384]{2,1,0:T(2,128)}, f32[4,2,384]{2,1,0:T(2,128)}, u32[]{:S(2)}, u32[]{:S(2)}) collective-permute-start(f32[4,2,384]{2,1,0:T(2,128)} %get-tuple-element.11.s0), channel_id=1, source_target_pairs={{0,28},{4,0},{8,4},{12,8},{16,12},{20,16},{24,20},{28,24},{1,29},{... | collective-permute-start | bytes 36872 | tf_op jit(solution)/shard_map/ppermute | solution.py:328
where the time goes:
time: 103 us; the launch traced here: 102 us
  Pallas kernels  35.9 us (35%)
  waiting for transfers between devices  24.8 us (24%)
  starting transfers between devices  23 us (22%)
  other arithmetic  10.9 us (11%)
  local copies, waits for them, and re-layouts  7.13 us (7%)
    ppermute x4, waiting for transfers between devices, passed_along(): return lax.ppermute(shard, axis, pairs)  16.4 us
    ppermute x4, starting transfers between devices, passed_along(): return lax.ppermute(shard, axis, pairs)  10.6 us
    pallas_call x1, Pallas kernels, key_grad_call(): pl.pallas_call(key_grad_kernel, name='key_grad', out_shape=(jax.ShapeDtyp...  9.3 us
    pallas_call x1, Pallas kernels, attend_call(): pl.pallas_call(attend_kernel, name='attend', out_shape=(jax.ShapeDtypeStr...  9.04 us
    ppermute x9, waiting for transfers between devices, swapped(): return lax.ppermute(shard, axis, [(i, i ^ bit) for i in range(length)])  8.35 us
    ppermute x9, starting transfers between devices, swapped(): return lax.ppermute(shard, axis, [(i, i ^ bit) for i in range(length)])  8.21 us
    pallas_call x1, Pallas kernels, query_grad_call(): pl.pallas_call(query_grad_kernel, name='query_grad', out_shape=jax.ShapeD...  6.9 us
    select_n x4, other arithmetic, pair(): return swapped(jnp.where(index % 2 == 0, from_even, from_odd), 'ctx', 1)  6.2 us
  transfers between devices with their start and end apart: 15, of which 6 were waited for; matrix products, arithmetic and copies ran while one was open for 12% of the time, Pallas kernels for 24%

commit v1 on v0

--- a/solution.py
+++ b/solution.py
@@ -16,7 +16,7 @@
 NEG_FILL = -1e30
 SCALE = 1.0 / math.sqrt(HD)
 LOG2E = 1.4426950408889634
-VMEM_BYTES = 67043328
+VMEM_BYTES = 32 << 20
 F32 = jnp.float32
 BF16 = jnp.bfloat16
 
@@ -36,10 +36,41 @@
     return lax.ppermute(shard, axis, [(i, i ^ bit) for i in range(length)])
 
 
-def window_starts(positions, offsets):
-    later, first = offsets[PREV:], offsets[:-PREV]
-    reached = jnp.where(later[None, :] <= positions[:, None], first[None, :], 0)
-    return jnp.max(reached, axis=1)
+def windows_kernel(base_ref, offsets_ref, col_ref, row_ref):
+    tiles, rows = row_ref.shape
+    lines = tiles * rows // HD
+    place = HD * lax.broadcasted_iota(jnp.int32, (lines, HD), 0) + lax.broadcasted_iota(
+        jnp.int32, (lines, HD), 1
+    )
+    position = base_ref[0] + place
+
+    def step(m, first):
+        return jnp.where(offsets_ref[m + PREV] <= position, offsets_ref[m], first)
+
+    first = lax.fori_loop(
+        0, offsets_ref.shape[0] - PREV, step, jnp.zeros_like(position), unroll=4
+    )
+    first = jnp.where(position < base_ref[1], first - base_ref[0], tiles * rows)
+    for line in range(lines):
+        tile, start = divmod(line * HD, rows)
+        row_ref[tile : tile + 1, start : start + HD] = first[line : line + 1, :]
+        if tile == 0:
+            spread = jnp.broadcast_to(first[line : line + 1, :], (HD, HD))
+            col_ref[start : start + HD, :] = spread.T
+
+
+def windows_call(base, offsets, rows):
+    return pl.pallas_call(
+        windows_kernel,
+        name="windows",
+        out_shape=(
+            jax.ShapeDtypeStruct((rows, HD), jnp.int32),
+            jax.ShapeDtypeStruct((REACH + 1, rows), jnp.int32),
+        ),
+        in_specs=[pl.BlockSpec(memory_space=pltpu.SMEM)] * 2,
+        compiler_params=pltpu.CompilerParams(vmem_limit_bytes=VMEM_BYTES),
+        cost_estimate=pl.CostEstimate(flops=1 << 20, bytes_accessed=1 << 18, transcendentals=0),
+    )(base, offsets)
 
 
 def mm(a, b, dims):
@@ -65,9 +96,10 @@
         out_shape=jax.ShapeDtypeStruct((rows, cols), BF16),
         grid_spec=pltpu.PrefetchScalarGridSpec(
             num_scalar_prefetch=1,
-            grid=(cols // HD,),
-            in_specs=[whole] * 4 + [pl.BlockSpec((HD, weight.shape[1]), lambda h, me: (h, 0))],
-            out_specs=pl.BlockSpec((rows, HD), lambda h, me: (0, h)),
+            grid=(cols // (2 * HD),),
+            in_specs=[whole] * 4
+            + [pl.BlockSpec((2 * HD, weight.shape[1]), lambda h, me: (h, 0))],
+            out_specs=pl.BlockSpec((rows, 2 * HD), lambda h, me: (0, h)),
         ),
         compiler_params=pltpu.CompilerParams(vmem_limit_bytes=VMEM_BYTES),
         cost_estimate=pl.CostEstimate(
@@ -91,8 +123,12 @@
         into[...] = odd_ref[...]
 
 
-def attend_kernel(odd_ref, lo_ref, q, k0, k2, v0, v2, r1, r2, r3, g, att_ref, prob_ref, stat_ref, k1, v1):
+def attend_kernel(
+    odd_ref, me_ref, lo_ref, q, k0, k2, v0, v2, r1, r2, r3, g, w_ref,
+    att_ref, prob_ref, stat_ref, sent_ref, mine_ref, far_ref, k1, v1,
+):
     rows = q.shape[0]
+    head = pl.program_id(0)
     pick(odd_ref[0], r2, r1, k1)
     pick(odd_ref[0], r3, r2, v1)
     keys, values = (k0, k1, k2), (v0, v1, v2)
@@ -103,47 +139,62 @@
         scores = []
         for tile, first, last, off in key_pieces(b, rows):
             raw = mm(qb, keys[tile][first:last, :], NT)
-            pos = off + first + lax.broadcasted_iota(jnp.int32, raw.shape, 1)
-            ok = pos >= lo
-            if tile == 0:
-                ok &= pos <= b * ROWS + lax.broadcasted_iota(jnp.int32, raw.shape, 0)
-            scores.append(jnp.where(ok, raw, NEG_FILL))
-        top = functools.reduce(
-            jnp.maximum, [jnp.max(s, axis=1, keepdims=True) for s in scores]
-        )
-        shift = top * (SCALE * LOG2E)
+            for c in range(0, last - first, HD):
+                part = raw[:, c : c + HD]
+                pos = off + first + c + lax.broadcasted_iota(jnp.int32, part.shape, 1)
+                ok = pos >= lo
+                if tile == 0 and first + c == b * ROWS:
+                    ok &= pos <= b * ROWS + lax.broadcasted_iota(jnp.int32, part.shape, 0)
+                scores.append(jnp.where(ok, part, NEG_FILL))
+        top = jnp.max(functools.reduce(jnp.maximum, scores), axis=1, keepdims=True)
+        shift = jnp.broadcast_to(top * (SCALE * LOG2E), (ROWS, HD))
         exps = [jnp.exp2(s * (SCALE * LOG2E) - shift) for s in scores]
-        total = functools.reduce(jnp.add, [jnp.sum(e, axis=1, keepdims=True) for e in exps])
-        inverse = 1.0 / total
+        total = jnp.sum(functools.reduce(jnp.add, exps), axis=1, keepdims=True)
+        inverse = jnp.broadcast_to(1.0 / total, (ROWS, HD))
         mixed = None
+        for n, e in enumerate(exps):
+            prob_ref[0, mine, n * HD : (n + 1) * HD] = (e * inverse).astype(BF16)
         column = 0
-        for e, (tile, first, last, off) in zip(exps, key_pieces(b, rows)):
-            prob = (e * inverse).astype(BF16)
-            prob_ref[0, mine, column : column + last - first] = prob
+        for tile, first, last, off in key_pieces(b, rows):
+            prob = prob_ref[0, mine, column : column + last - first]
             column += last - first
             part = mm(prob, values[tile][first:last, :], NN)
             mixed = part if mixed is None else mixed + part
         attended = mixed.astype(BF16)
-        att_ref[mine, :] = attended
+        att_ref[mine, pl.ds(pl.multiple_of(head * HD, HD), HD)] = attended
         delta = jnp.sum(attended.astype(F32) * g[mine, :].astype(F32), axis=1, keepdims=True)
         log_total = shift + jnp.log2(total)
         lane = lax.broadcasted_iota(jnp.int32, (ROWS, ROWS), 1)
         stats = jnp.where(lane == 0, log_total, delta).T
         stat_ref[0, :, mine] = stats[0:2, :]
 
+    @pl.when(head == pl.num_programs(0) - 1)
+    def _():
+        cols = att_ref.shape[1]
+
+        def project(group):
+            start = pl.multiple_of((me_ref[0] ^ group) * cols, cols)
+            return mm(att_ref[...], w_ref[:, pl.ds(start, cols)], NN)
+
+        sent_ref[:, 0:cols] = project(1).astype(BF16)
+        sent_ref[:, cols : 2 * cols] = project(3).astype(BF16)
+        far_ref[...] = project(2)
+        mine_ref[...] = project(0)
+
 
 def tile_specs(rows):
-    tile = pl.BlockSpec((rows, HD), lambda h, odd: (0, h))
-    on_odd = pl.BlockSpec((rows, HD), lambda h, odd: (0, h * odd[0]))
-    on_even = pl.BlockSpec((rows, HD), lambda h, odd: (0, h * (1 - odd[0])))
+    tile = pl.BlockSpec((rows, HD), lambda h, odd, *_: (0, h))
+    on_odd = pl.BlockSpec((rows, HD), lambda h, odd, *_: (0, h * odd[0]))
+    on_even = pl.BlockSpec((rows, HD), lambda h, odd, *_: (0, h * (1 - odd[0])))
     return tile, on_odd, on_even
 
 
-def attend_call(odd, lo, q, k0, k2, v0, v2, r1, r2, r3, g):
+def attend_call(odd, me, lo, q, k0, k2, v0, v2, r1, r2, r3, g, weight):
     rows, cols = q.shape
     heads = cols // HD
     tile, on_odd, on_even = tile_specs(rows)
     span = REACH * rows + ROWS
+    whole = pl.BlockSpec((rows, cols), lambda h, odd, me: (0, 0))
     return pl.pallas_call(
         attend_kernel,
         name="attend",
@@ -151,54 +202,33 @@
             jax.ShapeDtypeStruct((rows, cols), BF16),
             jax.ShapeDtypeStruct((heads, rows, span), BF16),
             jax.ShapeDtypeStruct((heads, 2, rows), F32),
+            jax.ShapeDtypeStruct((rows, 2 * cols), BF16),
+            jax.ShapeDtypeStruct((rows, cols), F32),
+            jax.ShapeDtypeStruct((rows, cols), F32),
         ),
         grid_spec=pltpu.PrefetchScalarGridSpec(
-            num_scalar_prefetch=1,
+            num_scalar_prefetch=2,
             grid=(heads,),
-            in_specs=[pl.BlockSpec((rows, 1), lambda h, odd: (0, 0))]
+            in_specs=[pl.BlockSpec((rows, HD), lambda h, odd, me: (0, 0))]
             + [tile] * 5
-            + [on_odd, tile, on_even, tile],
+            + [on_odd, tile, on_even, tile]
+            + [pl.BlockSpec(weight.shape, lambda h, odd, me: (0, 0))],
             out_specs=(
-                tile,
-                pl.BlockSpec((1, rows, span), lambda h, odd: (h, 0, 0)),
-                pl.BlockSpec((1, 2, rows), lambda h, odd: (h, 0, 0)),
+                whole,
+                pl.BlockSpec((1, rows, span), lambda h, odd, me: (h, 0, 0)),
+                pl.BlockSpec((1, 2, rows), lambda h, odd, me: (h, 0, 0)),
+                pl.BlockSpec((rows, 2 * cols), lambda h, odd, me: (0, 0)),
+                whole,
+                whole,
             ),
             scratch_shapes=[pltpu.VMEM((rows, HD), BF16)] * 2,
         ),
         compiler_params=pltpu.CompilerParams(vmem_limit_bytes=VMEM_BYTES),
         cost_estimate=pl.CostEstimate(
-            flops=4 * heads * rows * span * HD, bytes_accessed=8 << 20,
+            flops=8 * heads * rows * span * HD, bytes_accessed=12 << 20,
             transcendentals=heads * rows * span,
         ),
-    )(odd, lo, q, k0, k2, v0, v2, r1, r2, r3, g)
-
-
-def project_kernel(me_ref, a_ref, w_ref, out_ref):
-    out_ref[...] = mm(a_ref[...], w_ref[...], NN).astype(out_ref.dtype)
-
-
-def project_call(me, attended, weight, swaps, dtype):
-    rows, cols = attended.shape
-    base, step = swaps
-
-    return pl.pallas_call(
-        project_kernel,
-        name="project",
-        out_shape=jax.ShapeDtypeStruct((rows, 2 * cols), dtype),
-        grid_spec=pltpu.PrefetchScalarGridSpec(
-            num_scalar_prefetch=1,
-            grid=(2,),
-            in_specs=[
-                pl.BlockSpec((rows, cols), lambda s, me: (0, 0)),
-                pl.BlockSpec((cols, cols), lambda s, me: (0, me[0] ^ (base + step * s))),
-            ],
-            out_specs=pl.BlockSpec((rows, cols), lambda s, me: (0, s)),
-        ),
-        compiler_params=pltpu.CompilerParams(vmem_limit_bytes=VMEM_BYTES),
-        cost_estimate=pl.CostEstimate(
-            flops=4 * rows * cols * cols, bytes_accessed=3 << 20, transcendentals=0
-        ),
-    )(me, attended, weight)
+    )(odd, me, lo, q, k0, k2, v0, v2, r1, r2, r3, g, weight)
 
 
 def query_grad_kernel(odd_ref, prob_ref, att, k0, k2, v0, v2, r1, r2, r3, g, out_ref, k1, v1):
@@ -331,39 +361,33 @@
     cot_near = across(cotangent, 1)
     k2 = along(key_rows, 2)
     r1 = pair(key_rows, queries)
-    q2 = along(queries, -2)
     v2 = along(value_rows, 2)
     cot_both = across(cot_far, 1)
-
-    positions = base + jnp.arange((REACH + 1) * rows, dtype=jnp.int32)
-    lo = window_starts(positions, offsets) - base
-    lo = jnp.where(positions < count * rows, lo, (REACH + 1) * rows).reshape(REACH + 1, rows)
+    q2 = along(queries, -2)
+    r2 = pair(value_rows, k2)
 
     g = grad_out_call(me, (cotangent, cot_near, cot_far, cot_both), out_weight)
     g2 = along(g, -2)
-    r2 = pair(value_rows, k2)
+    bounds = jnp.stack([base, count * rows]).astype(jnp.int32)
+    lo_col, lo_row = windows_call(bounds, offsets, rows)
     r3 = pair(q2, v2)
     g1 = pair(g2, g)
 
-    attended, prob, stat = attend_call(
-        odd, lo[0].reshape(rows, 1), queries, key_rows, k2, value_rows, v2, r1, r2, r3, g
+    attended, prob, stat, sent, kept, kept_far = attend_call(
+        odd, me, lo_col, queries, key_rows, k2, value_rows, v2, r1, r2, r3, g, out_weight
     )
     stat1 = turned(stat, -1)
     stat2 = turned(stat, -2)
-
-    sent = project_call(me, attended, out_weight, (1, 2), BF16)
     came = across(sent, 1)
-    kept = project_call(me, attended, out_weight, (0, 2), F32)
-    both = kept + came.astype(F32)
-    mine, other = both[:, :cols], both[:, cols:].astype(BF16)
-    far = across(other, 2)
+    far = across((kept_far + came[:, cols:].astype(F32)).astype(BF16), 2)
+
     grad_queries = query_grad_call(
         odd, prob, attended, key_rows, k2, value_rows, v2, r1, r2, r3, g
     )
     grad_keys, grad_values = key_grad_call(
-        odd, lo, key_rows, value_rows, queries, q2, r1, r3, (g, g1, g2), (stat, stat1, stat2)
-    )
-    mixed = (mine + far.astype(F32)).astype(BF16)
+        odd, lo_row, key_rows, value_rows, queries, q2, r1, r3, (g, g1, g2), (stat, stat1, stat2)
+    )
+    mixed = (kept + came[:, :cols].astype(F32) + far.astype(F32)).astype(BF16)
     return (mixed, grad_queries, grad_keys, grad_values)
 
 

time: 103 us -> 90.3 us (0.88)
  Pallas kernels: 35.9 us -> 29 us
  local copies, waits for them, and re-layouts: 7.13 us -> 1.01 us
  other arithmetic: 10.9 us -> 6.57 us
  waiting for transfers between devices: 24.8 us -> 28.1 us
  starting transfers between devices: 23 us -> 24.4 us
    pallas_call x2 -> x1, Pallas kernels: 5.61 us -> 0.99 us  [windows_call(): pl.pallas_call(windows_kernel, name='windows', out_shape=(jax.ShapeDtypeS...]
    pallas_call x1, Pallas kernels: 5.04 us -> 2.49 us  [grad_out_call(): pl.pallas_call(grad_out_kernel, name='grad_out', out_shape=jax.ShapeDtype...]
    unnamed x16 -> x12, local copies, waits for them, and re-layouts: 3.4 us -> 1.01 us
    add x2 -> x0, other arithmetic: 1.82 us -> none  [the longest x1 1.82 us: layer(): both = kept + came.astype(F32)]
    ppermute x9, waiting for transfers between devices: 8.35 us -> 10.2 us  [swapped(): return lax.ppermute(shard, axis, [(i, i ^ bit) for i in range(length)])]
    slice x2 -> x0, local copies, waits for them, and re-layouts: 1.63 us -> none  [the longest x1 0.82 us: window_starts(): later, first = (offsets[PREV:], offsets[:-PREV])]
    ppermute x4, waiting for transfers between devices: 16.4 us -> 17.9 us  [passed_along(): return lax.ppermute(shard, axis, pairs)]
    sub x1 -> x0, local copies, waits for them, and re-layouts: 1.3 us -> none  [layer(): lo = window_starts(positions, offsets) - base]
  transfers between devices with their start and end apart: 15 -> 15, of which waited for: 6 -> 6; matrix products, arithmetic and copies ran while one was open for 12% -> 6% of each run, Pallas kernels for 24% -> 22%
where the time goes in v1:
time: 90.3 us; the launch traced here: 89.8 us
  Pallas kernels  29 us (32%)
  waiting for transfers between devices  28.1 us (31%)
  starting transfers between devices  24.4 us (27%)
  other arithmetic  6.57 us (7%)
  local copies, waits for them, and re-layouts  1.01 us (1%)
    ppermute x4, waiting for transfers between devices, passed_along(): return lax.ppermute(shard, axis, pairs)  17.9 us
    ppermute x4, starting transfers between devices, passed_along(): return lax.ppermute(shard, axis, pairs)  11.9 us
    ppermute x9, waiting for transfers between devices, swapped(): return lax.ppermute(shard, axis, [(i, i ^ bit) for i in range(length)])  10.2 us
    pallas_call x1, Pallas kernels, attend_call(): pl.pallas_call(attend_kernel, name='attend', out_shape=(jax.ShapeDtypeStr...  9.62 us
    pallas_call x1, Pallas kernels, key_grad_call(): pl.pallas_call(key_grad_kernel, name='key_grad', out_shape=(jax.ShapeDtyp...  9.26 us
    ppermute x9, starting transfers between devices, swapped(): return lax.ppermute(shard, axis, [(i, i ^ bit) for i in range(length)])  8.47 us
    pallas_call x1, Pallas kernels, query_grad_call(): pl.pallas_call(query_grad_kernel, name='query_grad', out_shape=jax.ShapeD...  6.6 us
    select_n x4, other arithmetic, pair(): return swapped(jnp.where(index % 2 == 0, from_even, from_odd), 'ctx', 1)  5.41 us
  transfers between devices with their start and end apart: 15, of which 6 were waited for; matrix products, arithmetic and copies ran while one was open for 6% of the time, Pallas kernels for 22%

profile of v1, /device:TPU:0, one launch (start us, length us, event | category | flops | bytes accessed | tf_op | source)
XLA Modules:
  0.0 89.8 jit_solution(6338817823071432121)
XLA Ops:
  0.7 5.1 %collective-permute-start = (bf16[384,512]{1,0:T(8,128)(2,1)}, bf16[384,512]{1,0:T(8,128)(2,1)S(1)}, u32[]{:S(2)}, u32[]{:S(2)}) collective-permute-start(bf16[384,512]{1,0:T(8,128)(2,1)} %k.1), channel_id=1, source_target_pairs={{0,8},{4,12},{8,16},{12,20},{16,24},{20,28},{1,9},{5,13},{9,17},{1... | collective-permute-start | bytes 1179656 | tf_op jit(solution)/shard_map/ppermute | solution.py:31
  5.8 0.1 collective-permute-start.6
  5.9 1.6 %collective-permute-start.7 = (bf16[384,512]{1,0:T(8,128)(2,1)}, bf16[384,512]{1,0:T(8,128)(2,1)}, u32[]{:S(2)}, u32[]{:S(2)}) collective-permute-start(bf16[384,512]{1,0:T(8,128)(2,1)} %c0.1), channel_id=1, source_target_pairs={{0,2},{1,3},{2,0},{3,1},{4,6},{5,7},{6,4},{7,5},{8,10},{9,11},{10,... | collective-permute-start | bytes 1179656 | tf_op jit(solution)/shard_map/ppermute | solution.py:36
  7.4 4.2 %collective-permute-start.1 = (bf16[384,512]{1,0:T(8,128)(2,1)}, bf16[384,512]{1,0:T(8,128)(2,1)}, u32[]{:S(2)}, u32[]{:S(2)}) collective-permute-start(bf16[384,512]{1,0:T(8,128)(2,1)} %v.1), channel_id=1, source_target_pairs={{0,8},{4,12},{8,16},{12,20},{16,24},{20,28},{1,9},{5,13},{9,17},{1... | collective-permute-start | bytes 1179656 | tf_op jit(solution)/shard_map/ppermute | solution.py:31
  11.6 1.3 %collective-permute-start.4 = (bf16[384,512]{1,0:T(8,128)(2,1)}, bf16[384,512]{1,0:T(8,128)(2,1)}, u32[]{:S(2)}, u32[]{:S(2)}) collective-permute-start(bf16[384,512]{1,0:T(8,128)(2,1)} %q0.1), channel_id=1, source_target_pairs={{8,0},{12,4},{16,8},{20,12},{24,16},{28,20},{9,1},{13,5},{17,9},{2... | collective-permute-start | bytes 1179656 | tf_op jit(solution)/shard_map/ppermute | solution.py:31
  12.9 1.8 %broadcast_select_fusion.3 = bf16[384,512]{1,0:T(8,128)(2,1)} fusion(bf16[384,512]{1,0:T(8,128)(2,1)} %k.1, bf16[384,512]{1,0:T(8,128)(2,1)} %q0.1, pred[]{:T(512)S(6)} %eq.12), kind=kLoop, calls=%fused_computation.5 | loop fusion | flops 196608 | bytes 1179649 | tf_op jit(solution)/shard_map/jit(_where)/select_n | solution.py:355
  14.7 0.8 collective-permute-done.k2
  15.6 1.5 %collective-permute-start.2 = (bf16[384,512]{1,0:T(8,128)(2,1)}, bf16[384,512]{1,0:T(8,128)(2,1)}, u32[]{:S(2)}, u32[]{:S(2)}) collective-permute-start(bf16[384,512]{1,0:T(8,128)(2,1)} %broadcast_select_fusion.3), channel_id=1, source_target_pairs={{0,4},{4,0},{8,12},{12,8},{16,20},{20,16},{24,28},{28,24},{1,5},{5... | collective-permute-start | bytes 1179656 | tf_op jit(solution)/shard_map/ppermute | solution.py:36
  17.1 1.8 %broadcast_select_fusion.2 = bf16[384,512]{1,0:T(8,128)(2,1)} fusion(bf16[384,512]{1,0:T(8,128)(2,1)} %v.1, bf16[384,512]{1,0:T(8,128)(2,1)S(1)} %collective-permute-done.k2, pred[]{:T(512)S(6)} %eq.12), kind=kLoop, calls=%fused_computation.4 | loop fusion | flops 196608 | bytes 1179649 | tf_op jit(solution)/shard_map/jit(_where)/select_n | solution.py:355
  18.9 4.0 %collective-permute-done.1.v2 = bf16[384,512]{1,0:T(8,128)(2,1)} collective-permute-done((bf16[384,512]{1,0:T(8,128)(2,1)}, bf16[384,512]{1,0:T(8,128)(2,1)}, u32[]{:S(2)}, u32[]{:S(2)}) %collective-permute-start.1) | collective-permute-done | bytes 393248 | tf_op jit(solution)/shard_map/ppermute | solution.py:31
  22.8 1.5 %collective-permute-start.3 = (bf16[384,512]{1,0:T(8,128)(2,1)}, bf16[384,512]{1,0:T(8,128)(2,1)}, u32[]{:S(2)}, u32[]{:S(2)}) collective-permute-start(bf16[384,512]{1,0:T(8,128)(2,1)} %broadcast_select_fusion.2), channel_id=1, source_target_pairs={{0,4},{4,0},{8,12},{12,8},{16,20},{20,16},{24,28},{28,24},{1,5},{5... | collective-permute-start | bytes 1179656 | tf_op jit(solution)/shard_map/ppermute | solution.py:36
  24.4 0.4 collective-permute-done.4.q2
  24.7 1.8 %broadcast_select_fusion.1 = bf16[384,512]{1,0:T(8,128)(2,1)} fusion(bf16[384,512]{1,0:T(8,128)(2,1)} %collective-permute-done.4.q2, bf16[384,512]{1,0:T(8,128)(2,1)} %collective-permute-done.1.v2, pred[]{:T(512)S(6)} %eq.12), kind=kLoop, calls=%fused_computation.3 | loop fusion | flops 196608 | bytes 1179649 | tf_op jit(solution)/shard_map/jit(_where)/select_n | solution.py:355
  26.5 1.5 %collective-permute-start.5 = (bf16[384,512]{1,0:T(8,128)(2,1)}, bf16[384,512]{1,0:T(8,128)(2,1)}, u32[]{:S(2)}, u32[]{:S(2)}) collective-permute-start(bf16[384,512]{1,0:T(8,128)(2,1)} %broadcast_select_fusion.1), channel_id=1, source_target_pairs={{0,4},{4,0},{8,12},{12,8},{16,20},{20,16},{24,28},{28,24},{1,5},{5... | collective-permute-start | bytes 1179656 | tf_op jit(solution)/shard_map/ppermute | solution.py:36
  28.0 0.1 pad_add_fusion.base_ref
  28.1 1.0 %windows.1 = (s32[384,128]{1,0:T(8,128)S(1)}, s32[3,384]{1,0:T(4,128)S(1)}) custom-call(s32[2]{0:T(128)S(1)} %pad_add_fusion.base_ref, s32[136]{0:T(256)S(1)} %copy-done.5), custom_call_target="tpu_custom_call" | custom-call | flops 1048576 | bytes 262144 | tf_op jit(solution)/shard_map/windows/pallas_call | solution.py:63
  29.2 1.0 %copy-done.4 = bf16[384,512]{1,0:T(8,128)(2,1)S(1)} copy-done((bf16[384,512]{1,0:T(8,128)(2,1)S(1)}, bf16[384,512]{1,0:T(8,128)(2,1)}, u32[]{:S(2)}) %copy-start.4) | copy-done | bytes 393240
  30.1 2.5 %grad_out.1.g.g0 = bf16[384,512]{1,0:T(8,128)(2,1)S(1)} custom-call(s32[1]{0:T(128)} %bitcast.1.me_ref, bf16[384,512]{1,0:T(8,128)(2,1)S(1)} %copy-done.4, bf16[384,512]{1,0:T(8,128)(2,1)} %collective-permute-done.6.c1, bf16[384,512]{1,0:T(8,128)(2,1)} %collective-permute-done.7.c2, bf16[384,512]{1,0:T(8,128)(2,1)} %collective-permute-done.8.c3, ...), custom_call_target="tpu_custom_call" | custom-call | flops 805306368 | bytes 6291456 | tf_op jit(solution)/shard_map/grad_out/pallas_call | solution.py:93
  32.7 2.9 %collective-permute-done.3.r2 = bf16[384,512]{1,0:T(8,128)(2,1)} collective-permute-done((bf16[384,512]{1,0:T(8,128)(2,1)}, bf16[384,512]{1,0:T(8,128)(2,1)}, u32[]{:S(2)}, u32[]{:S(2)}) %collective-permute-start.3) | collective-permute-done | bytes 393248 | tf_op jit(solution)/shard_map/ppermute | solution.py:36
  35.6 7.2 %collective-permute-done.5.r3 = bf16[384,512]{1,0:T(8,128)(2,1)} collective-permute-done((bf16[384,512]{1,0:T(8,128)(2,1)}, bf16[384,512]{1,0:T(8,128)(2,1)}, u32[]{:S(2)}, u32[]{:S(2)}) %collective-permute-start.5) | collective-permute-done | bytes 393248 | tf_op jit(solution)/shard_map/ppermute | solution.py:36
  42.8 9.6 %attend.1 = (bf16[384,512]{1,0:T(8,128)(2,1)S(1)}, bf16[4,384,896]{2,1,0:T(8,128)(2,1)S(1)}, f32[4,2,384]{2,1,0:T(2,128)S(1)}, bf16[384,1024]{1,0:T(8,128)(2,1)S...) custom-call(s32[1]{0:T(128)} %bitcast.odd_ref, s32[1]{0:T(128)} %bitcast.1.me_ref, ...), custom_call_target="tpu_custom_call" | custom-call | flops 1409286144 | bytes 12582912 | tf_op jit(solution)/shard_map/attend/pallas_call | solution.py:198
  52.4 0.1 collective-permute-start.9
  52.5 1.3 %collective-permute-start.11 = (bf16[384,512]{1,0:T(8,128)(2,1)S(1)}, bf16[384,512]{1,0:T(8,128)(2,1)S(1)}, u32[]{:S(2)}, u32[]{:S(2)}) collective-permute-start(bf16[384,512]{1,0:T(8,128)(2,1)S(1)} %grad_out.1.g.g0), channel_id=1, source_target_pairs={{8,0},{12,4},{16,8},{20,12},{24,16},{28,20},{9,1},{13,5},{17,9},{2... | collective-permute-start | bytes 1179656 | tf_op jit(solution)/shard_map/ppermute | solution.py:31
  53.8 12.7 %collective-permute-done.11.g2 = bf16[384,512]{1,0:T(8,128)(2,1)S(1)} collective-permute-done((bf16[384,512]{1,0:T(8,128)(2,1)S(1)}, bf16[384,512]{1,0:T(8,128)(2,1)S(1)}, u32[]{:S(2)}, u32[]{:S(2)}) %collective-permute-start.11) | collective-permute-done | bytes 393248 | tf_op jit(solution)/shard_map/ppermute | solution.py:31
  66.6 1.6 %collective-permute-start.12 = (bf16[384,512]{1,0:T(8,128)(2,1)S(1)}, bf16[384,512]{1,0:T(8,128)(2,1)S(1)}, u32[]{:S(2)}, u32[]{:S(2)}) collective-permute-start(bf16[384,512]{1,0:T(8,128)(2,1)S(1)} %broadcast_select_fusion), channel_id=1, source_target_pairs={{0,4},{4,0},{8,12},{12,8},{16,20},{20,16},{24,28},{28,24},{1,5},{5... | collective-permute-start | bytes 1179656 | tf_op jit(solution)/shard_map/ppermute | solution.py:36
  68.2 0.2 add_convert_fusion.1
  68.4 0.6 collective-permute-start.10
  69.0 1.5 %collective-permute-start.13 = (f32[4,2,384]{2,1,0:T(2,128)S(1)}, f32[4,2,384]{2,1,0:T(2,128)S(1)}, u32[]{:S(2)}, u32[]{:S(2)}) collective-permute-start(f32[4,2,384]{2,1,0:T(2,128)S(1)} %get-tuple-element.21.s0), channel_id=1, source_target_pairs={{0,28},{4,0},{8,4},{12,8},{16,12},{20,16},{24,20},{28,24},{1,29},{... | collective-permute-start | bytes 36872 | tf_op jit(solution)/shard_map/ppermute | solution.py:358
  70.5 2.5 %collective-permute-start.14 = (f32[4,2,384]{2,1,0:T(2,128)S(1)}, f32[4,2,384]{2,1,0:T(2,128)S(1)}, u32[]{:S(2)}, u32[]{:S(2)}) collective-permute-start(f32[4,2,384]{2,1,0:T(2,128)S(1)} %get-tuple-element.21.s0), channel_id=1, source_target_pairs={{0,24},{4,28},{8,0},{12,4},{16,8},{20,12},{24,16},{28,20},{1,25},{... | collective-permute-start | bytes 36872 | tf_op jit(solution)/shard_map/ppermute | solution.py:358
  73.0 6.6 %query_grad.1 = bf16[384,512]{1,0:T(8,128)(2,1)} custom-call(s32[1]{0:T(128)} %bitcast.odd_ref, bf16[4,384,896]{2,1,0:T(8,128)(2,1)S(1)} %get-tuple-element.18.prob_ref, bf16[384,512]{1,0:T(8,128)(2,1)S(1)} %get-tuple-element.19.att, bf16[384,512]{1,0:T(8,128)(2,1)S(1)} %copy-done.1, bf16[384,512]{1,0:T(8,128)(2,1)S(1)} %collective-permute-done.k2, ...), custom_call_target="tpu_custom_call" | custom-call | flops 704643072 | bytes 8388608 | tf_op jit(solution)/shard_map/query_grad/pallas_call | solution.py:260
  79.6 9.3 %key_grad.1 = (bf16[384,512]{1,0:T(8,128)(2,1)}, bf16[384,512]{1,0:T(8,128)(2,1)}) custom-call(s32[1]{0:T(128)} %bitcast.odd_ref, s32[3,384]{1,0:T(4,128)S(1)} %get-tuple-element.20.lo_ref, bf16[384,512]{1,0:T(8,128)(2,1)S(1)} %copy-done.1, bf16[384,512]{1,0:T(8,128)(2,1)S(1)} %copy-done.2, bf16[384,512]{1,0:T(8,128)(2,1)S(1)} %copy-done.3, ...), custom_call_target="tpu_custom_call" | custom-call | flops 1409286144 | bytes 5242880 | tf_op jit(solution)/shard_map/key_grad/pallas_call | solution.py:317
  88.8 0.9 %add_convert_fusion = bf16[384,512]{1,0:T(8,128)(2,1)} fusion(bf16[384,512]{1,0:T(8,128)(2,1)S(1)} %collective-permute-done.10, f32[384,512]{1,0:T(8,128)S(1)} %get-tuple-element.15, bf16[384,1024]{1,0:T(8,128)(2,1)S(1)} %collective-permute-done.9), kind=kLoop, calls=%fused_computation | loop fusion | flops 983040 | bytes 1966080 | tf_op jit(solution)/shard_map/convert_element_type | solution.py:390
  (22 shorter events, 0.1 us)
Async XLA Ops:
  0.6 27.5 %copy-start.5 = (s32[136]{0:T(256)S(1)}, s32[136]{0:T(256)}, u32[]{:S(2)}) copy-start(s32[136]{0:T(256)} %offsets_ref.1) | copy-start | bytes 1636
  0.6 28.5 %copy-start = (bf16[512,2048]{1,0:T(8,128)(2,1)S(1)}, bf16[512,2048]{1,0:T(8,128)(2,1)}, u32[]{:S(2)}) copy-start(bf16[512,2048]{1,0:T(8,128)(2,1)} %w_ref.3) | copy-start | bytes 6291460
  0.7 14.9 %collective-permute-start = (bf16[384,512]{1,0:T(8,128)(2,1)}, bf16[384,512]{1,0:T(8,128)(2,1)S(1)}, u32[]{:S(2)}, u32[]{:S(2)}) collective-permute-start(bf16[384,512]{1,0:T(8,128)(2,1)} %k.1), channel_id=1, source_target_pairs={{0,8},{4,12},{8,16},{12,20},{16,24},{20,28},{1,9},{5,13},{9,17},{1... | collective-permute-start | bytes 1179656 | tf_op jit(solution)/shard_map/ppermute | solution.py:31
  5.8 23.3 %collective-permute-start.6 = (bf16[384,512]{1,0:T(8,128)(2,1)}, bf16[384,512]{1,0:T(8,128)(2,1)}, u32[]{:S(2)}, u32[]{:S(2)}) collective-permute-start(bf16[384,512]{1,0:T(8,128)(2,1)} %c0.1), channel_id=1, source_target_pairs={{0,1},{1,0},{2,3},{3,2},{4,5},{5,4},{6,7},{7,6},{8,9},{9,8},{10,11... | collective-permute-start | bytes 1179656 | tf_op jit(solution)/shard_map/ppermute | solution.py:36
  5.9 18.5 %collective-permute-start.7 = (bf16[384,512]{1,0:T(8,128)(2,1)}, bf16[384,512]{1,0:T(8,128)(2,1)}, u32[]{:S(2)}, u32[]{:S(2)}) collective-permute-start(bf16[384,512]{1,0:T(8,128)(2,1)} %c0.1), channel_id=1, source_target_pairs={{0,2},{1,3},{2,0},{3,1},{4,6},{5,7},{6,4},{7,5},{8,10},{9,11},{10,... | collective-permute-start | bytes 1179656 | tf_op jit(solution)/shard_map/ppermute | solution.py:36
  7.4 15.4 %collective-permute-start.1 = (bf16[384,512]{1,0:T(8,128)(2,1)}, bf16[384,512]{1,0:T(8,128)(2,1)}, u32[]{:S(2)}, u32[]{:S(2)}) collective-permute-start(bf16[384,512]{1,0:T(8,128)(2,1)} %v.1), channel_id=1, source_target_pairs={{0,8},{4,12},{8,16},{12,20},{16,24},{20,28},{1,9},{5,13},{9,17},{1... | collective-permute-start | bytes 1179656 | tf_op jit(solution)/shard_map/ppermute | solution.py:31
  11.6 13.1 %collective-permute-start.4 = (bf16[384,512]{1,0:T(8,128)(2,1)}, bf16[384,512]{1,0:T(8,128)(2,1)}, u32[]{:S(2)}, u32[]{:S(2)}) collective-permute-start(bf16[384,512]{1,0:T(8,128)(2,1)} %q0.1), channel_id=1, source_target_pairs={{8,0},{12,4},{16,8},{20,12},{24,16},{28,20},{9,1},{13,5},{17,9},{2... | collective-permute-start | bytes 1179656 | tf_op jit(solution)/shard_map/ppermute | solution.py:31
  15.6 17.1 %collective-permute-start.2 = (bf16[384,512]{1,0:T(8,128)(2,1)}, bf16[384,512]{1,0:T(8,128)(2,1)}, u32[]{:S(2)}, u32[]{:S(2)}) collective-permute-start(bf16[384,512]{1,0:T(8,128)(2,1)} %broadcast_select_fusion.3), channel_id=1, source_target_pairs={{0,4},{4,0},{8,12},{12,8},{16,20},{20,16},{24,28},{28,24},{1,5},{5... | collective-permute-start | bytes 1179656 | tf_op jit(solution)/shard_map/ppermute | solution.py:36
  18.9 24.0 %copy-start.1 = (bf16[384,512]{1,0:T(8,128)(2,1)S(1)}, bf16[384,512]{1,0:T(8,128)(2,1)}, u32[]{:S(2)}) copy-start(bf16[384,512]{1,0:T(8,128)(2,1)} %k.1) | copy-start | bytes 1179652
  18.9 24.0 %copy-start.2 = (bf16[384,512]{1,0:T(8,128)(2,1)S(1)}, bf16[384,512]{1,0:T(8,128)(2,1)}, u32[]{:S(2)}) copy-start(bf16[384,512]{1,0:T(8,128)(2,1)} %v.1) | copy-start | bytes 1179652
  22.8 12.7 %collective-permute-start.3 = (bf16[384,512]{1,0:T(8,128)(2,1)}, bf16[384,512]{1,0:T(8,128)(2,1)}, u32[]{:S(2)}, u32[]{:S(2)}) collective-permute-start(bf16[384,512]{1,0:T(8,128)(2,1)} %broadcast_select_fusion.2), channel_id=1, source_target_pairs={{0,4},{4,0},{8,12},{12,8},{16,20},{20,16},{24,28},{28,24},{1,5},{5... | collective-permute-start | bytes 1179656 | tf_op jit(solution)/shard_map/ppermute | solution.py:36
  24.4 4.8 %collective-permute-start.8 = (bf16[384,512]{1,0:T(8,128)(2,1)}, bf16[384,512]{1,0:T(8,128)(2,1)}, u32[]{:S(2)}, u32[]{:S(2)}) collective-permute-start(bf16[384,512]{1,0:T(8,128)(2,1)} %collective-permute-done.7.c2), channel_id=1, source_target_pairs={{0,1},{1,0},{2,3},{3,2},{4,5},{5,4},{6,7},{7,6},{8,9},{9,8},{10,11... | collective-permute-start | bytes 1179656 | tf_op jit(solution)/shard_map/ppermute | solution.py:36
  26.5 16.3 %collective-permute-start.5 = (bf16[384,512]{1,0:T(8,128)(2,1)}, bf16[384,512]{1,0:T(8,128)(2,1)}, u32[]{:S(2)}, u32[]{:S(2)}) collective-permute-start(bf16[384,512]{1,0:T(8,128)(2,1)} %broadcast_select_fusion.1), channel_id=1, source_target_pairs={{0,4},{4,0},{8,12},{12,8},{16,20},{20,16},{24,28},{28,24},{1,5},{5... | collective-permute-start | bytes 1179656 | tf_op jit(solution)/shard_map/ppermute | solution.py:36
  28.0 14.8 %copy-start.3 = (bf16[384,512]{1,0:T(8,128)(2,1)S(1)}, bf16[384,512]{1,0:T(8,128)(2,1)}, u32[]{:S(2)}) copy-start(bf16[384,512]{1,0:T(8,128)(2,1)} %q0.1) | copy-start | bytes 1179652
  29.1 1.0 %copy-start.4 = (bf16[384,512]{1,0:T(8,128)(2,1)S(1)}, bf16[384,512]{1,0:T(8,128)(2,1)}, u32[]{:S(2)}) copy-start(bf16[384,512]{1,0:T(8,128)(2,1)} %c0.1) | copy-start | bytes 1179652
  52.4 15.8 %collective-permute-start.9 = (bf16[384,1024]{1,0:T(8,128)(2,1)S(1)}, bf16[384,1024]{1,0:T(8,128)(2,1)S(1)}, u32[]{:S(2)}, u32[]{:S(2)}) collective-permute-start(bf16[384,1024]{1,0:T(8,128)(2,1)S(1)} %get-tuple-element.16), channel_id=1, source_target_pairs={{0,1},{1,0},{2,3},{3,2},{4,5},{5,4},{6,7},{7,6},{8,9},{9,8},{10,11... | collective-permute-start | bytes 2359304 | tf_op jit(solution)/shard_map/ppermute | solution.py:36
  52.5 14.0 %collective-permute-start.11 = (bf16[384,512]{1,0:T(8,128)(2,1)S(1)}, bf16[384,512]{1,0:T(8,128)(2,1)S(1)}, u32[]{:S(2)}, u32[]{:S(2)}) collective-permute-start(bf16[384,512]{1,0:T(8,128)(2,1)S(1)} %grad_out.1.g.g0), channel_id=1, source_target_pairs={{8,0},{12,4},{16,8},{20,12},{24,16},{28,20},{9,1},{13,5},{17,9},{2... | collective-permute-start | bytes 1179656 | tf_op jit(solution)/shard_map/ppermute | solution.py:31
  66.6 13.0 %collective-permute-start.12 = (bf16[384,512]{1,0:T(8,128)(2,1)S(1)}, bf16[384,512]{1,0:T(8,128)(2,1)S(1)}, u32[]{:S(2)}, u32[]{:S(2)}) collective-permute-start(bf16[384,512]{1,0:T(8,128)(2,1)S(1)} %broadcast_select_fusion), channel_id=1, source_target_pairs={{0,4},{4,0},{8,12},{12,8},{16,20},{20,16},{24,28},{28,24},{1,5},{5... | collective-permute-start | bytes 1179656 | tf_op jit(solution)/shard_map/ppermute | solution.py:36
  68.4 20.5 %collective-permute-start.10 = (bf16[384,512]{1,0:T(8,128)(2,1)S(1)}, bf16[384,512]{1,0:T(8,128)(2,1)S(1)}, u32[]{:S(2)}, u32[]{:S(2)}) collective-permute-start(bf16[384,512]{1,0:T(8,128)(2,1)S(1)} %add_convert_fusion.1), channel_id=1, source_target_pairs={{0,2},{1,3},{2,0},{3,1},{4,6},{5,7},{6,4},{7,5},{8,10},{9,11},{10,... | collective-permute-start | bytes 1179656 | tf_op jit(solution)/shard_map/ppermute | solution.py:36
  69.0 10.6 %collective-permute-start.13 = (f32[4,2,384]{2,1,0:T(2,128)S(1)}, f32[4,2,384]{2,1,0:T(2,128)S(1)}, u32[]{:S(2)}, u32[]{:S(2)}) collective-permute-start(f32[4,2,384]{2,1,0:T(2,128)S(1)} %get-tuple-element.21.s0), channel_id=1, source_target_pairs={{0,28},{4,0},{8,4},{12,8},{16,12},{20,16},{24,20},{28,24},{1,29},{... | collective-permute-start | bytes 36872 | tf_op jit(solution)/shard_map/ppermute | solution.py:358
  70.5 9.1 %collective-permute-start.14 = (f32[4,2,384]{2,1,0:T(2,128)S(1)}, f32[4,2,384]{2,1,0:T(2,128)S(1)}, u32[]{:S(2)}, u32[]{:S(2)}) collective-permute-start(f32[4,2,384]{2,1,0:T(2,128)S(1)} %get-tuple-element.21.s0), channel_id=1, source_target_pairs={{0,24},{4,28},{8,0},{12,4},{16,8},{20,12},{24,16},{28,20},{1,25},{... | collective-permute-start | bytes 36872 | tf_op jit(solution)/shard_map/ppermute | solution.py:358

commit v2 on v1

--- a/solution.py
+++ b/solution.py
@@ -71,6 +71,14 @@
         compiler_params=pltpu.CompilerParams(vmem_limit_bytes=VMEM_BYTES),
         cost_estimate=pl.CostEstimate(flops=1 << 20, bytes_accessed=1 << 18, transcendentals=0),
     )(base, offsets)
+
+
+def in_hbm(*arrays):
+    return [pltpu.with_memory_space_constraint(x, pltpu.HBM) for x in arrays]
+
+
+def in_vmem(*arrays):
+    return [pltpu.with_memory_space_constraint(x, pltpu.VMEM) for x in arrays]
 
 
 def mm(a, b, dims):
@@ -105,7 +113,7 @@
         cost_estimate=pl.CostEstimate(
             flops=2 * rows * cols * weight.shape[1], bytes_accessed=6 << 20, transcendentals=0
         ),
-    )(me, *shards, weight)
+    )(me, *in_hbm(shards[0]), *in_vmem(*shards[1:]), *in_hbm(weight))
 
 
 def key_pieces(block, rows):
@@ -228,7 +236,7 @@
             flops=8 * heads * rows * span * HD, bytes_accessed=12 << 20,
             transcendentals=heads * rows * span,
         ),
-    )(odd, me, lo, q, k0, k2, v0, v2, r1, r2, r3, g, weight)
+    )(odd, me, lo, *in_hbm(q, k0), *in_vmem(k2), *in_hbm(v0), *in_vmem(v2, r1, r2, r3, g), *in_hbm(weight))
 
 
 def query_grad_kernel(odd_ref, prob_ref, att, k0, k2, v0, v2, r1, r2, r3, g, out_ref, k1, v1):
@@ -274,14 +282,17 @@
         cost_estimate=pl.CostEstimate(
             flops=4 * heads * rows * span * HD, bytes_accessed=8 << 20, transcendentals=0
         ),
-    )(odd, prob, att, k0, k2, v0, v2, r1, r2, r3, g)
+    )(odd, prob, att, *in_hbm(k0), *in_vmem(k2), *in_hbm(v0), *in_vmem(v2, r1, r2, r3, g))
 
 
 def key_grad_kernel(
-    odd_ref, lo_ref, k, v, q0, q2, r1, r3, g0, g1, g2, s0, s1, s2, dk_ref, dv_ref, q1
+    odd_ref, me_ref, lo_ref, k, v, q0, q2, r1, r3, g0, g1, g2, s0, s10, s11, s20, s21,
+    dk_ref, dv_ref, q1, s1, s2,
 ):
     rows = k.shape[0]
     pick(odd_ref[0], r1, r3, q1)
+    pick(me_ref[0] & 1, s10, s11, s1)
+    pick(me_ref[0] & 1, s20, s21, s2)
     queries, grads, stats = (q0, q1, q2), (g0, g1, g2), (s0, s1, s2)
     for b in range(rows // ROWS):
         mine = slice(b * ROWS, (b + 1) * ROWS)
@@ -308,33 +319,33 @@
         dv_ref[mine, :] = dv.astype(BF16)
 
 
-def key_grad_call(odd, lo, k, v, q0, q2, r1, r3, grads, stats):
+def key_grad_call(odd, me, lo, k, v, q0, q2, r1, r3, grads, stats):
     rows, cols = k.shape
     heads = cols // HD
     tile, on_odd, on_even = tile_specs(rows)
-    stat = pl.BlockSpec((1, 2, rows), lambda h, odd: (h, 0, 0))
+    stat = pl.BlockSpec((1, 2, rows), lambda h, odd, me: (h, 0, 0))
     span = REACH * rows + ROWS
     return pl.pallas_call(
         key_grad_kernel,
         name="key_grad",
         out_shape=(jax.ShapeDtypeStruct((rows, cols), BF16),) * 2,
         grid_spec=pltpu.PrefetchScalarGridSpec(
-            num_scalar_prefetch=1,
+            num_scalar_prefetch=2,
             grid=(heads,),
-            in_specs=[pl.BlockSpec((REACH + 1, rows), lambda h, odd: (0, 0))]
+            in_specs=[pl.BlockSpec((REACH + 1, rows), lambda h, odd, me: (0, 0))]
             + [tile] * 4
             + [on_even, on_odd]
             + [tile] * 3
-            + [stat] * 3,
+            + [stat] * 5,
             out_specs=(tile, tile),
-            scratch_shapes=[pltpu.VMEM((rows, HD), BF16)],
+            scratch_shapes=[pltpu.VMEM((rows, HD), BF16)] + [pltpu.VMEM((1, 2, rows), F32)] * 2,
         ),
         compiler_params=pltpu.CompilerParams(vmem_limit_bytes=VMEM_BYTES),
         cost_estimate=pl.CostEstimate(
             flops=8 * heads * rows * span * HD, bytes_accessed=5 << 20,
             transcendentals=heads * rows * span,
         ),
-    )(odd, lo, k, v, q0, q2, r1, r3, *grads, *stats)
+    )(odd, me, lo, *in_hbm(k, v, q0), *in_vmem(q2, r1, r3, *grads), *stats)
 
 
 def layer(queries, key_rows, value_rows, out_weight, cotangent, offsets):
@@ -354,8 +365,15 @@
     def pair(from_even, from_odd):
         return swapped(jnp.where(index % 2 == 0, from_even, from_odd), "ctx", 1)
 
-    def turned(shard, by):
-        return lax.ppermute(shard, "ctx", [(i, (i + by) % count) for i in range(count)])
+    def ringed(shard, by, bit):
+        groups = lax.axis_size("head")
+        pairs = []
+        for i in range(count):
+            for h in range(groups):
+                to = i - by if (h & 1) == bit else i + by
+                here = i * groups + h
+                pairs.append((here, to * groups + h if 0 <= to < count else here ^ 1))
+        return lax.ppermute(shard, ("ctx", "head"), pairs)
 
     cot_far = across(cotangent, 2)
     cot_near = across(cotangent, 1)
@@ -376,8 +394,7 @@
     attended, prob, stat, sent, kept, kept_far = attend_call(
         odd, me, lo_col, queries, key_rows, k2, value_rows, v2, r1, r2, r3, g, out_weight
     )
-    stat1 = turned(stat, -1)
-    stat2 = turned(stat, -2)
+    stats = [stat] + [ringed(stat, n, bit) for n in (1, 2) for bit in (0, 1)]
     came = across(sent, 1)
     far = across((kept_far + came[:, cols:].astype(F32)).astype(BF16), 2)
 
@@ -385,7 +402,7 @@
         odd, prob, attended, key_rows, k2, value_rows, v2, r1, r2, r3, g
     )
     grad_keys, grad_values = key_grad_call(
-        odd, lo_row, key_rows, value_rows, queries, q2, r1, r3, (g, g1, g2), (stat, stat1, stat2)
+        odd, me, lo_row, key_rows, value_rows, queries, q2, r1, r3, (g, g1, g2), stats
     )
     mixed = (kept + came[:, :cols].astype(F32) + far.astype(F32)).astype(BF16)
     return (mixed, grad_queries, grad_keys, grad_values)

time: 90.3 us -> 96.1 us (1.064)
  waiting for transfers between devices: 28.1 us -> 36.7 us
  starting transfers between devices: 24.4 us -> 23.2 us
  other arithmetic: 6.57 us -> 5.57 us
  local copies, waits for them, and re-layouts: 1.01 us -> 0.01 us
    ppermute x2 -> x4, waiting for transfers between devices: 0.01 us -> 6.41 us  [ringed(): return lax.ppermute(shard, ('ctx', 'head'), pairs)]
    ppermute x9, waiting for transfers between devices: 10.2 us -> 12.1 us  [swapped(): return lax.ppermute(shard, axis, [(i, i ^ bit) for i in range(length)])]
    unnamed x12 -> x2, local copies, waits for them, and re-layouts: 1.01 us -> 0.01 us
    select_n x4, other arithmetic: 5.41 us -> 4.42 us  [pair(): return swapped(jnp.where(index % 2 == 0, from_even, from_odd), 'ctx', 1)]
    ppermute x2 -> x4, starting transfers between devices: 3.98 us -> 3.75 us  [ringed(): return lax.ppermute(shard, ('ctx', 'head'), pairs)]
  transfers between devices with their start and end apart: 15 -> 17, of which waited for: 6 -> 6; matrix products, arithmetic and copies ran while one was open for 6% -> 5% of each run, Pallas kernels for 22% -> 20%
where the time goes in v2:
time: 96.1 us; the launch traced here: 95.7 us
  waiting for transfers between devices  36.7 us (38%)
  Pallas kernels  29.4 us (31%)
  starting transfers between devices  23.2 us (24%)
  other arithmetic  5.57 us (6%)
    ppermute x4, waiting for transfers between devices, passed_along(): return lax.ppermute(shard, axis, pairs)  18.3 us
    ppermute x9, waiting for transfers between devices, swapped(): return lax.ppermute(shard, axis, [(i, i ^ bit) for i in range(length)])  12.1 us
    ppermute x4, starting transfers between devices, passed_along(): return lax.ppermute(shard, axis, pairs)  11 us
    pallas_call x1, Pallas kernels, attend_call(): pl.pallas_call(attend_kernel, name='attend', out_shape=(jax.ShapeDtypeStr...  10.2 us
    pallas_call x1, Pallas kernels, key_grad_call(): pl.pallas_call(key_grad_kernel, name='key_grad', out_shape=(jax.ShapeDtyp...  9.24 us
    ppermute x9, starting transfers between devices, swapped(): return lax.ppermute(shard, axis, [(i, i ^ bit) for i in range(length)])  8.45 us
    ppermute x4, waiting for transfers between devices, ringed(): return lax.ppermute(shard, ('ctx', 'head'), pairs)  6.41 us
    pallas_call x1, Pallas kernels, query_grad_call(): pl.pallas_call(query_grad_kernel, name='query_grad', out_shape=jax.ShapeD...  6.37 us
  transfers between devices with their start and end apart: 17, of which 6 were waited for; matrix products, arithmetic and copies ran while one was open for 5% of the time, Pallas kernels for 20%

profile of v2, /device:TPU:0, one launch (start us, length us, event | category | flops | bytes accessed | tf_op | source)
XLA Modules:
  0.0 95.7 jit_solution(5634951873031578775)
XLA Ops:
  0.6 5.0 %collective-permute-start = (bf16[384,512]{1,0:T(8,128)(2,1)}, bf16[384,512]{1,0:T(8,128)(2,1)S(1)}, u32[]{:S(2)}, u32[]{:S(2)}) collective-permute-start(bf16[384,512]{1,0:T(8,128)(2,1)} %k.1), channel_id=1, source_target_pairs={{0,8},{4,12},{8,16},{12,20},{16,24},{20,28},{1,9},{5,13},{9,17},{1... | collective-permute-start | bytes 1179656 | tf_op jit(solution)/shard_map/ppermute | solution.py:31
  5.6 0.1 collective-permute-start.6
  5.7 1.6 %collective-permute-start.7 = (bf16[384,512]{1,0:T(8,128)(2,1)}, bf16[384,512]{1,0:T(8,128)(2,1)S(1)}, u32[]{:S(2)}, u32[]{:S(2)}) collective-permute-start(bf16[384,512]{1,0:T(8,128)(2,1)} %c0.1), channel_id=1, source_target_pairs={{0,2},{1,3},{2,0},{3,1},{4,6},{5,7},{6,4},{7,5},{8,10},{9,11},{10,... | collective-permute-start | bytes 1179656 | tf_op jit(solution)/shard_map/ppermute | solution.py:36
  7.3 3.5 %collective-permute-start.1 = (bf16[384,512]{1,0:T(8,128)(2,1)}, bf16[384,512]{1,0:T(8,128)(2,1)S(1)}, u32[]{:S(2)}, u32[]{:S(2)}) collective-permute-start(bf16[384,512]{1,0:T(8,128)(2,1)} %v.1), channel_id=1, source_target_pairs={{0,8},{4,12},{8,16},{12,20},{16,24},{20,28},{1,9},{5,13},{9,17},{1... | collective-permute-start | bytes 1179656 | tf_op jit(solution)/shard_map/ppermute | solution.py:31
  10.8 1.3 %collective-permute-start.4 = (bf16[384,512]{1,0:T(8,128)(2,1)}, bf16[384,512]{1,0:T(8,128)(2,1)S(1)}, u32[]{:S(2)}, u32[]{:S(2)}) collective-permute-start(bf16[384,512]{1,0:T(8,128)(2,1)} %q0.1), channel_id=1, source_target_pairs={{8,0},{12,4},{16,8},{20,12},{24,16},{28,20},{9,1},{13,5},{17,9},{2... | collective-permute-start | bytes 1179656 | tf_op jit(solution)/shard_map/ppermute | solution.py:31
  12.1 1.8 %broadcast_select_fusion.3 = bf16[384,512]{1,0:T(8,128)(2,1)} fusion(bf16[384,512]{1,0:T(8,128)(2,1)} %k.1, bf16[384,512]{1,0:T(8,128)(2,1)} %q0.1, pred[]{:T(512)S(6)} %eq.12), kind=kLoop, calls=%fused_computation.5 | loop fusion | flops 196608 | bytes 1179649 | tf_op jit(solution)/shard_map/jit(_where)/select_n | solution.py:366
  13.9 1.5 %collective-permute-done.k2 = bf16[384,512]{1,0:T(8,128)(2,1)S(1)} collective-permute-done((bf16[384,512]{1,0:T(8,128)(2,1)}, bf16[384,512]{1,0:T(8,128)(2,1)S(1)}, u32[]{:S(2)}, u32[]{:S(2)}) %collective-permute-start) | collective-permute-done | bytes 393248 | tf_op jit(solution)/shard_map/ppermute | solution.py:31
  15.4 1.5 %collective-permute-start.2 = (bf16[384,512]{1,0:T(8,128)(2,1)}, bf16[384,512]{1,0:T(8,128)(2,1)S(1)}, u32[]{:S(2)}, u32[]{:S(2)}) collective-permute-start(bf16[384,512]{1,0:T(8,128)(2,1)} %broadcast_select_fusion.3), channel_id=1, source_target_pairs={{0,4},{4,0},{8,12},{12,8},{16,20},{20,16},{24,28},{28,24},{1,5},{5... | collective-permute-start | bytes 1179656 | tf_op jit(solution)/shard_map/ppermute | solution.py:36
  16.9 1.8 %broadcast_select_fusion.2 = bf16[384,512]{1,0:T(8,128)(2,1)} fusion(bf16[384,512]{1,0:T(8,128)(2,1)} %v.1, bf16[384,512]{1,0:T(8,128)(2,1)S(1)} %collective-permute-done.k2, pred[]{:T(512)S(6)} %eq.12), kind=kLoop, calls=%fused_computation.4 | loop fusion | flops 196608 | bytes 1179649 | tf_op jit(solution)/shard_map/jit(_where)/select_n | solution.py:366
  18.7 4.0 %collective-permute-done.1.v2 = bf16[384,512]{1,0:T(8,128)(2,1)S(1)} collective-permute-done((bf16[384,512]{1,0:T(8,128)(2,1)}, bf16[384,512]{1,0:T(8,128)(2,1)S(1)}, u32[]{:S(2)}, u32[]{:S(2)}) %collective-permute-start.1) | collective-permute-done | bytes 393248 | tf_op jit(solution)/shard_map/ppermute | solution.py:31
  22.7 1.5 %collective-permute-start.3 = (bf16[384,512]{1,0:T(8,128)(2,1)}, bf16[384,512]{1,0:T(8,128)(2,1)S(1)}, u32[]{:S(2)}, u32[]{:S(2)}) collective-permute-start(bf16[384,512]{1,0:T(8,128)(2,1)} %broadcast_select_fusion.2), channel_id=1, source_target_pairs={{0,4},{4,0},{8,12},{12,8},{16,20},{20,16},{24,28},{28,24},{1,5},{5... | collective-permute-start | bytes 1179656 | tf_op jit(solution)/shard_map/ppermute | solution.py:36
  24.2 0.8 broadcast_select_fusion.1
  25.0 1.0 %collective-permute-start.5 = (bf16[384,512]{1,0:T(8,128)(2,1)}, bf16[384,512]{1,0:T(8,128)(2,1)S(1)}, u32[]{:S(2)}, u32[]{:S(2)}) collective-permute-start(bf16[384,512]{1,0:T(8,128)(2,1)} %broadcast_select_fusion.1), channel_id=1, source_target_pairs={{0,4},{4,0},{8,12},{12,8},{16,20},{20,16},{24,28},{28,24},{1,5},{5... | collective-permute-start | bytes 1179656 | tf_op jit(solution)/shard_map/ppermute | solution.py:36
  26.1 0.1 pad_add_fusion.base_ref
  26.1 1.0 %windows.1 = (s32[384,128]{1,0:T(8,128)S(1)}, s32[3,384]{1,0:T(4,128)S(1)}) custom-call(s32[2]{0:T(128)S(1)} %pad_add_fusion.base_ref, s32[136]{0:T(256)S(1)} %copy-done), custom_call_target="tpu_custom_call" | custom-call | flops 1048576 | bytes 262144 | tf_op jit(solution)/shard_map/windows/pallas_call | solution.py:63
  27.2 2.6 %grad_out.1.g.g0 = bf16[384,512]{1,0:T(8,128)(2,1)S(1)} custom-call(s32[1]{0:T(128)} %bitcast.1.me_ref, bf16[384,512]{1,0:T(8,128)(2,1)} %c0.1, bf16[384,512]{1,0:T(8,128)(2,1)S(1)} %collective-permute-done.6.c1, bf16[384,512]{1,0:T(8,128)(2,1)S(1)} %collective-permute-done.7.c2, bf16[384,512]{1,0:T(8,128)(2,1)S(1)} %collective-permute-done.8.c3, ...), custom_call_target="tpu_custom_call" | custom-call | flops 805306368 | bytes 6291456 | tf_op jit(solution)/shard_map/grad_out/pallas_call | solution.py:101
  29.8 5.1 %collective-permute-done.3.r2 = bf16[384,512]{1,0:T(8,128)(2,1)S(1)} collective-permute-done((bf16[384,512]{1,0:T(8,128)(2,1)}, bf16[384,512]{1,0:T(8,128)(2,1)S(1)}, u32[]{:S(2)}, u32[]{:S(2)}) %collective-permute-start.3) | collective-permute-done | bytes 393248 | tf_op jit(solution)/shard_map/ppermute | solution.py:36
  34.9 6.9 %collective-permute-done.5.r3 = bf16[384,512]{1,0:T(8,128)(2,1)S(1)} collective-permute-done((bf16[384,512]{1,0:T(8,128)(2,1)}, bf16[384,512]{1,0:T(8,128)(2,1)S(1)}, u32[]{:S(2)}, u32[]{:S(2)}) %collective-permute-start.5) | collective-permute-done | bytes 393248 | tf_op jit(solution)/shard_map/ppermute | solution.py:36
  41.8 10.2 %attend.1 = (bf16[384,512]{1,0:T(8,128)(2,1)S(1)}, bf16[4,384,896]{2,1,0:T(8,128)(2,1)S(1)}, f32[4,2,384]{2,1,0:T(2,128)S(1)}, bf16[384,1024]{1,0:T(8,128)(2,1)S...) custom-call(s32[1]{0:T(128)} %bitcast.odd_ref, s32[1]{0:T(128)} %bitcast.1.me_ref, ...), custom_call_target="tpu_custom_call" | custom-call | flops 1409286144 | bytes 12582912 | tf_op jit(solution)/shard_map/attend/pallas_call | solution.py:206
  52.0 0.1 collective-permute-start.9
  52.1 1.3 %collective-permute-start.11 = (bf16[384,512]{1,0:T(8,128)(2,1)S(1)}, bf16[384,512]{1,0:T(8,128)(2,1)S(1)}, u32[]{:S(2)}, u32[]{:S(2)}) collective-permute-start(bf16[384,512]{1,0:T(8,128)(2,1)S(1)} %grad_out.1.g.g0), channel_id=1, source_target_pairs={{8,0},{12,4},{16,8},{20,12},{24,16},{28,20},{9,1},{13,5},{17,9},{2... | collective-permute-start | bytes 1179656 | tf_op jit(solution)/shard_map/ppermute | solution.py:31
  53.4 12.7 %collective-permute-done.11.g2 = bf16[384,512]{1,0:T(8,128)(2,1)S(1)} collective-permute-done((bf16[384,512]{1,0:T(8,128)(2,1)S(1)}, bf16[384,512]{1,0:T(8,128)(2,1)S(1)}, u32[]{:S(2)}, u32[]{:S(2)}) %collective-permute-start.11) | collective-permute-done | bytes 393248 | tf_op jit(solution)/shard_map/ppermute | solution.py:31
  66.1 0.1 broadcast_select_fusion
  66.2 1.6 %collective-permute-start.12 = (bf16[384,512]{1,0:T(8,128)(2,1)S(1)}, bf16[384,512]{1,0:T(8,128)(2,1)S(1)}, u32[]{:S(2)}, u32[]{:S(2)}) collective-permute-start(bf16[384,512]{1,0:T(8,128)(2,1)S(1)} %broadcast_select_fusion), channel_id=1, source_target_pairs={{0,4},{4,0},{8,12},{12,8},{16,20},{20,16},{24,28},{28,24},{1,5},{5... | collective-permute-start | bytes 1179656 | tf_op jit(solution)/shard_map/ppermute | solution.py:36
  67.8 0.1 add_convert_fusion.1
  67.9 1.1 %collective-permute-start.10 = (bf16[384,512]{1,0:T(8,128)(2,1)S(1)}, bf16[384,512]{1,0:T(8,128)(2,1)S(1)}, u32[]{:S(2)}, u32[]{:S(2)}) collective-permute-start(bf16[384,512]{1,0:T(8,128)(2,1)S(1)} %add_convert_fusion.1), channel_id=1, source_target_pairs={{0,2},{1,3},{2,0},{3,1},{4,6},{5,7},{6,4},{7,5},{8,10},{9,11},{10,... | collective-permute-start | bytes 1179656 | tf_op jit(solution)/shard_map/ppermute | solution.py:36
  69.0 2.0 %collective-permute-start.14 = (f32[4,2,384]{2,1,0:T(2,128)S(1)}, f32[4,2,384]{2,1,0:T(2,128)S(1)}, u32[]{:S(2)}, u32[]{:S(2)}) collective-permute-start(f32[4,2,384]{2,1,0:T(2,128)S(1)} %get-tuple-element.21.s0), channel_id=1, source_target_pairs={{0,4},{1,0},{2,6},{3,2},{4,8},{5,1},{6,10},{7,3},{8,12},{9,5},{10,... | collective-permute-start | bytes 36872 | tf_op jit(solution)/shard_map/ppermute | solution.py:376
  71.0 6.4 %collective-permute-done.13.s10 = f32[4,2,384]{2,1,0:T(2,128)S(1)} collective-permute-done((f32[4,2,384]{2,1,0:T(2,128)S(1)}, f32[4,2,384]{2,1,0:T(2,128)S(1)}, u32[]{:S(2)}, u32[]{:S(2)}) %collective-permute-start.13) | collective-permute-done | bytes 12320 | tf_op jit(solution)/shard_map/ppermute | solution.py:376
  77.4 1.7 %collective-permute-start.16 = (f32[4,2,384]{2,1,0:T(2,128)S(1)}, f32[4,2,384]{2,1,0:T(2,128)S(1)}, u32[]{:S(2)}, u32[]{:S(2)}) collective-permute-start(f32[4,2,384]{2,1,0:T(2,128)S(1)} %get-tuple-element.21.s0), channel_id=1, source_target_pairs={{0,8},{1,0},{2,10},{3,2},{4,12},{5,4},{6,14},{7,6},{8,16},{9,1},{1... | collective-permute-start | bytes 36872 | tf_op jit(solution)/shard_map/ppermute | solution.py:376
  79.1 6.4 %query_grad.1 = bf16[384,512]{1,0:T(8,128)(2,1)} custom-call(s32[1]{0:T(128)} %bitcast.odd_ref, bf16[4,384,896]{2,1,0:T(8,128)(2,1)S(1)} %get-tuple-element.18.prob_ref, bf16[384,512]{1,0:T(8,128)(2,1)S(1)} %get-tuple-element.19.att, bf16[384,512]{1,0:T(8,128)(2,1)} %k.1, bf16[384,512]{1,0:T(8,128)(2,1)S(1)} %collective-permute-done.k2, bf16[384,512]{1,0:T(8,128)(2,1)} %v.1, ...), custom_call_target="tpu_custom_call" | custom-call | flops 704643072 | bytes 8388608 | tf_op jit(solution)/shard_map/query_grad/pallas_call | solution.py:268
  85.5 9.2 %key_grad.1 = (bf16[384,512]{1,0:T(8,128)(2,1)}, bf16[384,512]{1,0:T(8,128)(2,1)}) custom-call(s32[1]{0:T(128)} %bitcast.odd_ref, s32[1]{0:T(128)} %bitcast.1.me_ref, s32[3,384]{1,0:T(4,128)S(1)} %get-tuple-element.20.lo_ref, bf16[384,512]{1,0:T(8,128)(2,1)} %k.1, bf16[384,512]{1,0:T(8,128)(2,1)} %v.1, bf16[384,512]{1,0:T(8,128)(2,1)} %q0.1, ...), custom_call_target="tpu_custom_call" | custom-call | flops 1409286144 | bytes 5242880 | tf_op jit(solution)/shard_map/key_grad/pallas_call | solution.py:328
  94.8 0.9 add_convert_fusion
  (16 shorter events, 0.0 us)
Async XLA Ops:
  0.6 25.5 %copy-start = (s32[136]{0:T(256)S(1)}, s32[136]{0:T(256)}, u32[]{:S(2)}) copy-start(s32[136]{0:T(256)} %offsets_ref.1) | copy-start | bytes 1636
  0.6 14.8 %collective-permute-start = (bf16[384,512]{1,0:T(8,128)(2,1)}, bf16[384,512]{1,0:T(8,128)(2,1)S(1)}, u32[]{:S(2)}, u32[]{:S(2)}) collective-permute-start(bf16[384,512]{1,0:T(8,128)(2,1)} %k.1), channel_id=1, source_target_pairs={{0,8},{4,12},{8,16},{12,20},{16,24},{20,28},{1,9},{5,13},{9,17},{1... | collective-permute-start | bytes 1179656 | tf_op jit(solution)/shard_map/ppermute | solution.py:31
  5.6 21.5 %collective-permute-start.6 = (bf16[384,512]{1,0:T(8,128)(2,1)}, bf16[384,512]{1,0:T(8,128)(2,1)S(1)}, u32[]{:S(2)}, u32[]{:S(2)}) collective-permute-start(bf16[384,512]{1,0:T(8,128)(2,1)} %c0.1), channel_id=1, source_target_pairs={{0,1},{1,0},{2,3},{3,2},{4,5},{5,4},{6,7},{7,6},{8,9},{9,8},{10,11... | collective-permute-start | bytes 1179656 | tf_op jit(solution)/shard_map/ppermute | solution.py:36
  5.7 18.5 %collective-permute-start.7 = (bf16[384,512]{1,0:T(8,128)(2,1)}, bf16[384,512]{1,0:T(8,128)(2,1)S(1)}, u32[]{:S(2)}, u32[]{:S(2)}) collective-permute-start(bf16[384,512]{1,0:T(8,128)(2,1)} %c0.1), channel_id=1, source_target_pairs={{0,2},{1,3},{2,0},{3,1},{4,6},{5,7},{6,4},{7,5},{8,10},{9,11},{10,... | collective-permute-start | bytes 1179656 | tf_op jit(solution)/shard_map/ppermute | solution.py:36
  7.3 15.4 %collective-permute-start.1 = (bf16[384,512]{1,0:T(8,128)(2,1)}, bf16[384,512]{1,0:T(8,128)(2,1)S(1)}, u32[]{:S(2)}, u32[]{:S(2)}) collective-permute-start(bf16[384,512]{1,0:T(8,128)(2,1)} %v.1), channel_id=1, source_target_pairs={{0,8},{4,12},{8,16},{12,20},{16,24},{20,28},{1,9},{5,13},{9,17},{1... | collective-permute-start | bytes 1179656 | tf_op jit(solution)/shard_map/ppermute | solution.py:31
  10.8 13.5 %collective-permute-start.4 = (bf16[384,512]{1,0:T(8,128)(2,1)}, bf16[384,512]{1,0:T(8,128)(2,1)S(1)}, u32[]{:S(2)}, u32[]{:S(2)}) collective-permute-start(bf16[384,512]{1,0:T(8,128)(2,1)} %q0.1), channel_id=1, source_target_pairs={{8,0},{12,4},{16,8},{20,12},{24,16},{28,20},{9,1},{13,5},{17,9},{2... | collective-permute-start | bytes 1179656 | tf_op jit(solution)/shard_map/ppermute | solution.py:31
  15.4 14.3 %collective-permute-start.2 = (bf16[384,512]{1,0:T(8,128)(2,1)}, bf16[384,512]{1,0:T(8,128)(2,1)S(1)}, u32[]{:S(2)}, u32[]{:S(2)}) collective-permute-start(bf16[384,512]{1,0:T(8,128)(2,1)} %broadcast_select_fusion.3), channel_id=1, source_target_pairs={{0,4},{4,0},{8,12},{12,8},{16,20},{20,16},{24,28},{28,24},{1,5},{5... | collective-permute-start | bytes 1179656 | tf_op jit(solution)/shard_map/ppermute | solution.py:36
  22.7 12.2 %collective-permute-start.3 = (bf16[384,512]{1,0:T(8,128)(2,1)}, bf16[384,512]{1,0:T(8,128)(2,1)S(1)}, u32[]{:S(2)}, u32[]{:S(2)}) collective-permute-start(bf16[384,512]{1,0:T(8,128)(2,1)} %broadcast_select_fusion.2), channel_id=1, source_target_pairs={{0,4},{4,0},{8,12},{12,8},{16,20},{20,16},{24,28},{28,24},{1,5},{5... | collective-permute-start | bytes 1179656 | tf_op jit(solution)/shard_map/ppermute | solution.py:36
  24.2 2.9 %collective-permute-start.8 = (bf16[384,512]{1,0:T(8,128)(2,1)S(1)}, bf16[384,512]{1,0:T(8,128)(2,1)S(1)}, u32[]{:S(2)}, u32[]{:S(2)}) collective-permute-start(bf16[384,512]{1,0:T(8,128)(2,1)S(1)} %collective-permute-done.7.c2), channel_id=1, source_target_pairs={{0,1},{1,0},{2,3},{3,2},{4,5},{5,4},{6,7},{7,6},{8,9},{9,8},{10,11... | collective-permute-start | bytes 1179656 | tf_op jit(solution)/shard_map/ppermute | solution.py:36
  25.0 16.8 %collective-permute-start.5 = (bf16[384,512]{1,0:T(8,128)(2,1)}, bf16[384,512]{1,0:T(8,128)(2,1)S(1)}, u32[]{:S(2)}, u32[]{:S(2)}) collective-permute-start(bf16[384,512]{1,0:T(8,128)(2,1)} %broadcast_select_fusion.1), channel_id=1, source_target_pairs={{0,4},{4,0},{8,12},{12,8},{16,20},{20,16},{24,28},{28,24},{1,5},{5... | collective-permute-start | bytes 1179656 | tf_op jit(solution)/shard_map/ppermute | solution.py:36
  52.0 15.8 %collective-permute-start.9 = (bf16[384,1024]{1,0:T(8,128)(2,1)S(1)}, bf16[384,1024]{1,0:T(8,128)(2,1)S(1)}, u32[]{:S(2)}, u32[]{:S(2)}) collective-permute-start(bf16[384,1024]{1,0:T(8,128)(2,1)S(1)} %get-tuple-element.16), channel_id=1, source_target_pairs={{0,1},{1,0},{2,3},{3,2},{4,5},{5,4},{6,7},{7,6},{8,9},{9,8},{10,11... | collective-permute-start | bytes 2359304 | tf_op jit(solution)/shard_map/ppermute | solution.py:36
  52.1 14.0 %collective-permute-start.11 = (bf16[384,512]{1,0:T(8,128)(2,1)S(1)}, bf16[384,512]{1,0:T(8,128)(2,1)S(1)}, u32[]{:S(2)}, u32[]{:S(2)}) collective-permute-start(bf16[384,512]{1,0:T(8,128)(2,1)S(1)} %grad_out.1.g.g0), channel_id=1, source_target_pairs={{8,0},{12,4},{16,8},{20,12},{24,16},{28,20},{9,1},{13,5},{17,9},{2... | collective-permute-start | bytes 1179656 | tf_op jit(solution)/shard_map/ppermute | solution.py:31
  66.2 19.4 %collective-permute-start.12 = (bf16[384,512]{1,0:T(8,128)(2,1)S(1)}, bf16[384,512]{1,0:T(8,128)(2,1)S(1)}, u32[]{:S(2)}, u32[]{:S(2)}) collective-permute-start(bf16[384,512]{1,0:T(8,128)(2,1)S(1)} %broadcast_select_fusion), channel_id=1, source_target_pairs={{0,4},{4,0},{8,12},{12,8},{16,20},{20,16},{24,28},{28,24},{1,5},{5... | collective-permute-start | bytes 1179656 | tf_op jit(solution)/shard_map/ppermute | solution.py:36
  67.9 26.9 %collective-permute-start.10 = (bf16[384,512]{1,0:T(8,128)(2,1)S(1)}, bf16[384,512]{1,0:T(8,128)(2,1)S(1)}, u32[]{:S(2)}, u32[]{:S(2)}) collective-permute-start(bf16[384,512]{1,0:T(8,128)(2,1)S(1)} %add_convert_fusion.1), channel_id=1, source_target_pairs={{0,2},{1,3},{2,0},{3,1},{4,6},{5,7},{6,4},{7,5},{8,10},{9,11},{10,... | collective-permute-start | bytes 1179656 | tf_op jit(solution)/shard_map/ppermute | solution.py:36
  69.0 8.4 %collective-permute-start.13 = (f32[4,2,384]{2,1,0:T(2,128)S(1)}, f32[4,2,384]{2,1,0:T(2,128)S(1)}, u32[]{:S(2)}, u32[]{:S(2)}) collective-permute-start(f32[4,2,384]{2,1,0:T(2,128)S(1)} %get-tuple-element.21.s0), channel_id=1, source_target_pairs={{0,1},{1,5},{2,3},{3,7},{4,0},{5,9},{6,2},{7,11},{8,4},{9,13},{10,... | collective-permute-start | bytes 36872 | tf_op jit(solution)/shard_map/ppermute | solution.py:376
  69.0 16.5 %collective-permute-start.14 = (f32[4,2,384]{2,1,0:T(2,128)S(1)}, f32[4,2,384]{2,1,0:T(2,128)S(1)}, u32[]{:S(2)}, u32[]{:S(2)}) collective-permute-start(f32[4,2,384]{2,1,0:T(2,128)S(1)} %get-tuple-element.21.s0), channel_id=1, source_target_pairs={{0,4},{1,0},{2,6},{3,2},{4,8},{5,1},{6,10},{7,3},{8,12},{9,5},{10,... | collective-permute-start | bytes 36872 | tf_op jit(solution)/shard_map/ppermute | solution.py:376
  71.0 14.5 %collective-permute-start.15 = (f32[4,2,384]{2,1,0:T(2,128)S(1)}, f32[4,2,384]{2,1,0:T(2,128)S(1)}, u32[]{:S(2)}, u32[]{:S(2)}) collective-permute-start(f32[4,2,384]{2,1,0:T(2,128)S(1)} %get-tuple-element.21.s0), channel_id=1, source_target_pairs={{0,1},{1,9},{2,3},{3,11},{4,5},{5,13},{6,7},{7,15},{8,0},{9,17},{1... | collective-permute-start | bytes 36872 | tf_op jit(solution)/shard_map/ppermute | solution.py:376
  77.4 8.1 %collective-permute-start.16 = (f32[4,2,384]{2,1,0:T(2,128)S(1)}, f32[4,2,384]{2,1,0:T(2,128)S(1)}, u32[]{:S(2)}, u32[]{:S(2)}) collective-permute-start(f32[4,2,384]{2,1,0:T(2,128)S(1)} %get-tuple-element.21.s0), channel_id=1, source_target_pairs={{0,8},{1,0},{2,10},{3,2},{4,12},{5,4},{6,14},{7,6},{8,16},{9,1},{1... | collective-permute-start | bytes 36872 | tf_op jit(solution)/shard_map/ppermute | solution.py:376
